TPU v7x, 32 devices: a whole 2x2x4 slice. The times are simulated.
32 devices in a mesh: member: 8 (over z, core), basin: 4 (over y, x).
Axes of the slice: x: 2, y: 2, z: 4, core: 2. Of those that a mesh axis runs over, the one named last changes fastest.
Arguments:
- prior_params: float32 [256, 8, 512], P('member', None, 'basin'), may hold values from -3 to 3
- lateral_flow: float32 [256, 2, 65536], P('member', None, 'basin'), may hold values from 0.2 to 2
- inflow_start: float32 [65536], P('basin'), may hold values from 0.5 to 4
- outflow_start: float32 [65536], P('basin'), may hold values from 0.5 to 4
- reach_count: int32 [512], P('basin'), may hold values from 64 to 128
- downstream: int32 [512], P('basin'), may hold values from 0 to 63
- gauge_reach: int32 [2048], P('basin'), may hold values from 0 to 16383
- observed: float32 [2, 2048], P(None, 'basin'), may hold values from 0.5 to 4
- obs_var: float32 [2, 2048], P(None, 'basin'), may hold values from 0.02 to 0.5
- obs_noise: float32 [256, 2, 2048], P('member', None, 'basin'), may hold values from -4 to 4
Outputs:
- posterior: float32 [256, 8, 512], P('member', None, 'basin')
- predicted: float32 [256, 2, 2048], P('member', None, 'basin')
All inputs are finite; a program needn't handle non-finite values.
Results may differ from a plain program's by a relative error of at most 0.0003.
Values sent between devices are 32-bit elements; how exact they have to be, the bound alone decides.
A program may use at most 128 MiB of HBM per device.

v0:
```python
import functools
import math

import jax
import jax.numpy as jnp
from jax import lax
import numpy as np
from jax.experimental import pallas as pl
from jax.experimental.pallas import tpu as pltpu
from jax.sharding import PartitionSpec as P

LANES = 128
BLK_LEV = 64
exact_mode = lax.Precision.HIGHEST
VMEM = pltpu.VMEM
SMEM = pltpu.SMEM
MESH = pl.DeviceIdType.MESH


def vmem_spec():
    return pl.BlockSpec(memory_space=VMEM)


def smem_spec():
    return pl.BlockSpec(memory_space=SMEM)


def exchange_body(axis, n, spread_out, x_ref, o_ref, send_sem, recv_sem, own_sem):
    me = lax.axis_index(axis)
    barrier = pltpu.get_barrier_semaphore()
    for i in range(1, n):
        pl.semaphore_signal(
            barrier, inc=1, device_id={axis: lax.rem(me + i, n)}, device_id_type=MESH
        )
    pl.semaphore_wait(barrier, n - 1)
    copies = []
    for i in range(1, n):
        peer = lax.rem(me + i, n)
        copies.append(
            pltpu.make_async_remote_copy(
                src_ref=x_ref.at[peer] if spread_out else x_ref,
                dst_ref=o_ref.at[me],
                send_sem=send_sem.at[i - 1],
                recv_sem=recv_sem.at[i - 1],
                device_id={axis: peer},
                device_id_type=MESH,
            )
        )
    for copy in copies:
        copy.start()
    own = pltpu.make_async_copy(x_ref.at[me] if spread_out else x_ref, o_ref.at[me], own_sem)
    own.start()
    own.wait()
    for copy in copies:
        copy.wait()


def exchange(x, axis, collective_id, spread_out=False):
    n = lax.axis_size(axis)
    shape = x.shape if spread_out else (n,) + x.shape
    return pl.pallas_call(
        functools.partial(exchange_body, axis, n, spread_out),
        out_shape=jax.ShapeDtypeStruct(shape, x.dtype),
        in_specs=[vmem_spec()],
        out_specs=vmem_spec(),
        scratch_shapes=[
            pltpu.SemaphoreType.DMA((n - 1,)),
            pltpu.SemaphoreType.DMA((n - 1,)),
            pltpu.SemaphoreType.DMA,
        ],
        compiler_params=pltpu.CompilerParams(collective_id=collective_id, has_side_effects=True),
        name=f"exchange_{collective_id}",
    )(x)


def doubling_bits(n):
    bits = []
    bit = n // 2
    while bit:
        bits.append(bit)
        bit //= 2
    return bits


def observed_body(
    hours, n_basin, n, x_ref, o_ref, land_ref, part_send, part_recv, send_sem, recv_sem
):
    basin = lax.axis_index("basin")
    me = lax.axis_index("member")
    partners = [me + bit * (1 - 2 * lax.rem(me // bit, 2)) for bit in doubling_bits(n)]
    barrier = pltpu.get_barrier_semaphore()
    for i in range(1, n_basin):
        pl.semaphore_signal(
            barrier, inc=1, device_id={"basin": lax.rem(basin + i, n_basin)}, device_id_type=MESH
        )
    for partner in partners:
        pl.semaphore_signal(barrier, inc=1, device_id={"member": partner}, device_id_type=MESH)
    pl.semaphore_wait(barrier, n_basin - 1 + len(partners))
    parts = []
    for i in range(1, n_basin):
        peer = lax.rem(basin + i, n_basin)
        parts.append(
            pltpu.make_async_remote_copy(
                src_ref=x_ref.at[peer], dst_ref=land_ref.at[i - 1],
                send_sem=part_send.at[i - 1], recv_sem=part_recv.at[i - 1],
                device_id={"basin": peer}, device_id_type=MESH,
            )
        )
    for copy in parts:
        copy.start()
    for copy in parts:
        copy.wait()
    flows = x_ref[basin]
    for i in range(1, n_basin):
        flows = flows + land_ref[i - 1]
    pred = inverse_sinh(flows)
    rows = o_ref.shape[1]
    gauges = x_ref.shape[2]
    for h in range(hours):
        o_ref[0, :, h * gauges : (h + 1) * gauges] = pred[h * rows : (h + 1) * rows]

    copies = {}
    for p in range(n):
        if p:
            copies[p].wait_recv()
        for k, partner in enumerate(partners):
            to = 2**k + p
            if p < 2**k:
                copies[to] = pltpu.make_async_remote_copy(
                    src_ref=o_ref.at[p], dst_ref=o_ref.at[to],
                    send_sem=send_sem.at[to - 1], recv_sem=recv_sem.at[to - 1],
                    device_id={"member": partner}, device_id_type=MESH,
                )
                copies[to].start()
    for p in range(1, n):
        copies[p].wait_send()


def observed_gather(parts, hours, collective_id):
    n = lax.axis_size("member")
    n_basin = lax.axis_size("basin")
    rows, gauges = parts.shape[1] // hours, parts.shape[2]
    return pl.pallas_call(
        functools.partial(observed_body, hours, n_basin, n),
        out_shape=jax.ShapeDtypeStruct((n, rows, hours * gauges), parts.dtype),
        in_specs=[vmem_spec()],
        out_specs=vmem_spec(),
        scratch_shapes=[
            VMEM((n_basin - 1,) + parts.shape[1:], parts.dtype),
            pltpu.SemaphoreType.DMA((n_basin - 1,)),
            pltpu.SemaphoreType.DMA((n_basin - 1,)),
            pltpu.SemaphoreType.DMA((n - 1,)),
            pltpu.SemaphoreType.DMA((n - 1,)),
        ],
        compiler_params=pltpu.CompilerParams(collective_id=collective_id, has_side_effects=True),
        name=f"observed_{collective_id}",
    )(parts)


def sum_body(axis, n, x_ref, o_ref, land_ref, sem1, sem2, sem3, sem4):
    me = lax.axis_index(axis)
    barrier = pltpu.get_barrier_semaphore()
    for i in range(1, n):
        pl.semaphore_signal(
            barrier, inc=1, device_id={axis: lax.rem(me + i, n)}, device_id_type=MESH
        )
    pl.semaphore_wait(barrier, n - 1)
    copies = []
    for i in range(1, n):
        peer = lax.rem(me + i, n)
        copies.append(
            pltpu.make_async_remote_copy(
                src_ref=x_ref.at[peer], dst_ref=land_ref.at[i - 1],
                send_sem=sem1.at[i - 1], recv_sem=sem2.at[i - 1],
                device_id={axis: peer}, device_id_type=MESH,
            )
        )
    for copy in copies:
        copy.start()
    for copy in copies:
        copy.wait()
    total = x_ref[me]
    for i in range(1, n):
        total = total + land_ref[i - 1]
    o_ref[me] = total
    copies = []
    for i in range(1, n):
        copies.append(
            pltpu.make_async_remote_copy(
                src_ref=o_ref.at[me], dst_ref=o_ref.at[me],
                send_sem=sem3.at[i - 1], recv_sem=sem4.at[i - 1],
                device_id={axis: lax.rem(me + i, n)}, device_id_type=MESH,
            )
        )
    for copy in copies:
        copy.start()
    for copy in copies:
        copy.wait()


def sum_over(x, axis, collective_id):
    n = lax.axis_size(axis)
    return pl.pallas_call(
        functools.partial(sum_body, axis, n),
        out_shape=jax.ShapeDtypeStruct(x.shape, x.dtype),
        in_specs=[vmem_spec()],
        out_specs=vmem_spec(),
        scratch_shapes=[VMEM((n - 1,) + x.shape[1:], x.dtype)]
        + [pltpu.SemaphoreType.DMA((n - 1,))] * 4,
        compiler_params=pltpu.CompilerParams(collective_id=collective_id, has_side_effects=True),
        name=f"sum_{collective_id}",
    )(x)


def permuted_step(held, axis, bit):
    n = lax.axis_size(axis)
    other = lax.ppermute(held, axis, [(i, i ^ bit) for i in range(n)])
    return jnp.concatenate([held, other], 0)


def route_body(
    seg_count, level_count, members, gauges, hours, param_count,
    basin_ref, down_ref, count_ref, gauge_row_ref, gauge_pack_ref,
    meta_ref, prior_ref, cos_ref, pin_ref, pout_ref, lat_hbm,
    out_ref,
    up_ref, flow_ref, row_ref, now_ref, back_ref, carry_ref, par_ref, raw_ref, ready_ref, sem,
):
    first = basin_ref[0]
    lev = BLK_LEV
    seg_blocks = level_count * lev
    rows = members
    packs = LANES // members
    shape = (rows, LANES)
    lane = lax.broadcasted_iota(jnp.int32, shape, 1)
    place = (lane // members) * members + lax.broadcasted_iota(jnp.int32, shape, 0)

    chunks = sem.shape[0]
    chunk_rows = seg_blocks * hours // chunks

    def fetch(c, m):
        span = pl.ds(c * chunk_rows, chunk_rows)
        return pltpu.make_async_copy(lat_hbm.at[m, span], raw_ref.at[span, m], sem.at[c, m])

    for c in range(chunks):
        for m in range(members):
            fetch(c, m).start()

    def clear(i, _):
        up_ref[i] = jnp.zeros((2 * rows, LANES), jnp.float32)
        return 0

    lax.fori_loop(0, 2 * lev, clear, 0, unroll=8)

    def turned(values):
        return jnp.concatenate([values] * packs, axis=0).T

    def coefficients(seg, _):
        storage = 0.02 + 0.1 * jax.nn.sigmoid(meta_ref[seg, :members, :])
        weighting = 0.2 * jax.nn.sigmoid(meta_ref[seg, members : 2 * members, :])
        den = storage * (1.0 - weighting) + 0.5
        span = pl.ds(pl.multiple_of(seg * seg_blocks, seg_blocks), seg_blocks)
        now_ref[span, :] = turned((0.5 - storage * weighting) / den)
        back_ref[span, :] = turned((0.5 + storage * weighting) / den)
        carry_ref[span, :] = turned((storage * (1.0 - weighting) - 0.5) / den)
        return 0

    lax.fori_loop(first, seg_count, coefficients, 0)
    for k in range(param_count - 2):
        par_ref[k] = turned(0.2 * prior_ref[:, 2 + k, :])

    def place_group(tiles):
        flat = jnp.concatenate(tiles, axis=0).T
        strips = [flat[q * rows : (q + 1) * rows] for q in range(packs)]
        made = []
        for i in range(packs):
            total = None
            for q in range(packs):
                shift = ((q - i) * members) % LANES
                piece = pltpu.roll(strips[q], shift, 1) if shift else strips[q]
                total = piece if total is None else jnp.where(lane // members == q, piece, total)
            made.append(total)
        return made

    def relayout(group, _):
        base = group * packs
        for h in range(hours):
            tiles = [raw_ref[(base + i) * hours + h] for i in range(packs)]
            for i, tile in enumerate(place_group(tiles)):
                ready_ref[base + i, h] = tile
        for n, ref in enumerate((pin_ref, pout_ref)):
            tiles = [
                jnp.broadcast_to(ref[pl.ds(base + i, 1), :], shape) for i in range(packs)
            ]
            for i, tile in enumerate(place_group(tiles)):
                ready_ref[base + i, hours + n] = tile
        return 0

    chunk_groups = seg_blocks // packs // chunks
    for c in range(chunks):
        for m in range(members):
            fetch(c, m).wait()
        lax.fori_loop(c * chunk_groups, (c + 1) * chunk_groups, relayout, 0, unroll=2)

    def sweep(seg, level, parity, own):
        def block(j, _):
            here = level * lev + j
            b = seg * seg_blocks + here
            live = place < count_ref[b]
            now = now_ref[pl.ds(b, 1), :]
            back = back_ref[pl.ds(b, 1), :]
            carry = carry_ref[pl.ds(b, 1), :]
            if own:
                expo = cos_ref[0] * par_ref[0, pl.ds(here, 1), :]
                for k in range(1, cos_ref.shape[0]):
                    expo = expo + cos_ref[k] * par_ref[k, pl.ds(here, 1), :]
                scale = jnp.exp(expo)
                add0 = ready_ref[here, 0] * scale
                add1 = ready_ref[here, 1] * scale
                if level > 0:
                    add0 = add0 + up_ref[parity * lev + j, :rows]
                    add1 = add1 + up_ref[parity * lev + j, rows:]
                in0 = jnp.where(live, add0, 0.0)
                in1 = jnp.where(live, add1, 0.0)
                start = back * ready_ref[here, 2] + carry * ready_ref[here, 3]
                out0 = now * in0 + jnp.where(live, start, 0.0)
            else:
                in0 = jnp.where(live, up_ref[parity * lev + j, :rows], 0.0)
                in1 = jnp.where(live, up_ref[parity * lev + j, rows:], 0.0)
                out0 = now * in0
            out1 = now * in1 + back * in0 + carry * out0
            up_ref[parity * lev + j] = jnp.zeros((2 * rows, LANES), jnp.float32)
            flow_ref[pl.ds(here * 2 * rows, rows), :] = out0
            flow_ref[pl.ds(here * 2 * rows + rows, rows), :] = out1
            target = (1 - parity) * lev + down_ref[b]
            up_ref[target, :rows] += out0
            up_ref[target, rows:] += out1
            return 0

        lax.fori_loop(0, lev, block, 0, unroll=4)

    fold = lax.broadcasted_iota(jnp.int32, shape, 0) == lane % members
    fold = fold.astype(jnp.float32)
    one_lane = lax.broadcasted_iota(jnp.int32, (1, LANES), 1) // members

    def observe(seg):
        first_gauge = seg * gauges

        def one(g, _):
            row = gauge_row_ref[first_gauge + g]
            keep = one_lane == gauge_pack_ref[first_gauge + g]
            row_ref[pl.ds(g, 1), :] = jnp.where(keep, flow_ref[pl.ds(row, 1), :], 0.0)
            row_ref[pl.ds(gauges + g, 1), :] = jnp.where(
                keep, flow_ref[pl.ds(row + rows, 1), :], 0.0
            )
            return 0

        lax.fori_loop(0, gauges, one, 0, unroll=8)
        for h in range(2):
            out_ref[seg, h * members : (h + 1) * members, :] = lax.dot_general(
                fold, row_ref[h * gauges : (h + 1) * gauges, :], (((1,), (1,)), ((), ())),
                precision=exact_mode, preferred_element_type=jnp.float32,
            )

    def nothing(seg, _):
        out_ref[seg] = jnp.zeros(out_ref.shape[1:], jnp.float32)
        return 0

    lax.fori_loop(0, first, nothing, 0)
    for level in range(level_count):
        sweep(first, level, level % 2, True)
    observe(first)

    def later(seg, _):
        for level in range(level_count):
            sweep(seg, level, level % 2, False)
        observe(seg)
        return 0

    lax.fori_loop(first + 1, seg_count, later, 0)


def invert_small(d, panel=8):
    size = d.shape[0]
    lane = lax.broadcasted_iota(jnp.int32, d.shape, 1)
    sub = lax.broadcasted_iota(jnp.int32, d.shape, 0)
    for base in range(0, size, panel):
        cols = [jnp.broadcast_to(d[:, base + i : base + i + 1], d.shape) for i in range(panel)]
        for i in range(panel):
            j = base + i
            pivot = cols[i]
            inv = 1.0 / pivot[j : j + 1, :]
            row = jnp.where(lane[:1] == j, 1.0, d[j : j + 1, :]) * inv
            d = jnp.where(sub == j, row, jnp.where(lane == j, 0.0, d) - pivot * row)
            for l in range(i + 1, panel):
                factor = pivot[base + l : base + l + 1, :] * inv
                cols[l] = jnp.where(sub == j, factor, cols[l] - pivot * factor)
    return d


def exact_dot(a, b):
    return jnp.dot(a, b, precision=exact_mode, preferred_element_type=jnp.float32)


def solve_body(n, size, sums_ref, out_ref, a_ref, l_ref):
    total = n * size
    sub = lax.broadcasted_iota(jnp.int32, (total, total), 0)
    lane = lax.broadcasted_iota(jnp.int32, (total, total), 1)
    a_ref[...] = sums_ref[:total, :] + jnp.where(lane == sub, 1.0, 0.0)
    out_ref[...] = sums_ref[total : total + size, :].T
    for k in range(n):
        span = slice(k * size, (k + 1) * size)
        left = (k * size // LANES) * LANES
        inverse = invert_small(a_ref[span, span])
        right = exact_dot(inverse, out_ref[span, :])
        l_ref[...] = a_ref[:, span]
        l_ref[span, :] = jnp.zeros((size, size), jnp.float32)
        column = l_ref[...]
        if k < n - 1:
            top = exact_dot(inverse, a_ref[span, left:])
            a_ref[:, left:] -= exact_dot(column, top)
            a_ref[span, left:] = top
        out_ref[...] -= exact_dot(column, right)
        out_ref[span, :] = right


def inverse_sinh(values):
    return jnp.log(values + jnp.sqrt(values * values + 1.0))


def shards(
    prior_params, lateral_flow, inflow_start, outflow_start, reach_count, downstream,
    gauge_reach, observed, obs_var, obs_noise,
):
    md, param_count, block_dev = prior_params.shape
    hours = lateral_flow.shape[1]
    gauges = gauge_reach.shape[0]
    basins = lax.axis_size("basin")
    n_member = lax.axis_size("member")
    members = md * n_member
    level_count = block_dev // BLK_LEV
    packs = LANES // md
    f32 = jnp.float32

    prior_steps = doubling_bits(n_member)
    held = permuted_step(prior_params[None], "member", prior_steps[0])

    gauge_rows = gauges // block_dev
    extra = -(md * 2 + 2 + gauge_rows) % 8
    meta = jnp.concatenate(
        [
            prior_params[:, 0, :],
            prior_params[:, 1, :],
            downstream.astype(f32)[None],
            reach_count.astype(f32)[None],
            gauge_reach.astype(f32).reshape(-1, block_dev),
            jnp.zeros((extra, block_dev), f32),
        ],
        0,
    )
    meta_all = exchange(meta, "basin", 1)
    down_all = meta_all[:, md * 2].reshape(-1).astype(jnp.int32)
    count_all = meta_all[:, md * 2 + 1].reshape(-1).astype(jnp.int32)
    slots = meta_all[:, md * 2 + 2 : md * 2 + 2 + gauge_rows].reshape(-1).astype(jnp.int32)
    gauge_row = slots // LANES * (hours * md) + slots % md
    gauge_pack = slots % LANES // md

    modes = param_count - 2
    lane_pos = np.arange(LANES)
    cosine = np.cos(math.pi * np.arange(modes)[:, None] * (lane_pos[None, :] + 0.5) / LANES)
    cosine = np.swapaxes(cosine.reshape(modes, packs, md), 1, 2)
    cosine = jnp.asarray(np.repeat(cosine, md, axis=2), f32)

    lateral = lateral_flow.reshape(md, hours, block_dev, LANES)
    lateral = jnp.swapaxes(lateral, 1, 2).reshape(md, block_dev * hours, LANES)
    held, meta_all = lax.optimization_barrier((held, meta_all))
    for bit in prior_steps[1:-1]:
        held = permuted_step(held, "member", bit)
    basin_idx = lax.axis_index("basin").astype(jnp.int32).reshape(1)
    seg_coef = VMEM((basins * block_dev, LANES), f32)

    parts = pl.pallas_call(
        functools.partial(route_body, basins, level_count, md, gauges, hours, param_count),
        out_shape=jax.ShapeDtypeStruct((basins, 2 * md, gauges), f32),
        in_specs=[smem_spec()] * 5 + [vmem_spec()] * 5 + [pl.BlockSpec(memory_space=pl.ANY)],
        out_specs=vmem_spec(),
        scratch_shapes=[
            VMEM((2 * BLK_LEV, 2 * md, LANES), f32),
            VMEM((block_dev * 2 * md, LANES), f32),
            VMEM((2 * gauges, LANES), f32),
            seg_coef,
            seg_coef,
            seg_coef,
            VMEM((modes, block_dev, LANES), f32),
            VMEM((block_dev * hours, md, LANES), f32),
            VMEM((block_dev, hours + 2, md, LANES), f32),
            pltpu.SemaphoreType.DMA((4, md)),
        ],
        cost_estimate=pl.CostEstimate(
            flops=40_000_000, bytes_accessed=60_000_000, transcendentals=0
        ),
        name="route",
    )(
        basin_idx, down_all, count_all, gauge_row, gauge_pack, meta_all, prior_params, cosine,
        inflow_start.reshape(block_dev, LANES), outflow_start.reshape(block_dev, LANES), lateral,
    )
    parts, held = lax.optimization_barrier((parts, held))
    held = permuted_step(held, "member", prior_steps[-1])
    prior_all = held.reshape(members, param_count * block_dev)
    gathered = observed_gather(parts, hours, 2)
    flat = gathered[0]
    predicted = flat.reshape(md, hours, gauges)
    pred_all = gathered.reshape(members, hours * gauges)

    spread = jnp.sqrt(obs_var).reshape(1, -1)
    spread_root = math.sqrt(members - 1.0)
    noise = jnp.concatenate([obs_noise[:, h] for h in range(hours)], axis=1)
    innovation = (observed.reshape(1, -1) + 2.0 * spread * noise - flat) / (2.0 * spread)
    mean_pred = jnp.sum(pred_all, 0, keepdims=True) / members
    scaled_all = (pred_all - mean_pred) / (spread_root * (2.0 * spread))
    row_count = members + md
    extra = -row_count % (8 * basins)
    both = jnp.concatenate([scaled_all, innovation, jnp.zeros((extra, flat.shape[1]), f32)], 0)
    part = lax.dot_general(
        both, scaled_all, (((1,), (1,)), ((), ())),
        precision=exact_mode, preferred_element_type=f32,
    )
    sums = sum_over(part.reshape(basins, -1, members), "basin", 4).reshape(-1, members)
    gain = pl.pallas_call(
        functools.partial(solve_body, n_member, md),
        out_shape=jax.ShapeDtypeStruct((members, md), f32),
        in_specs=[vmem_spec()],
        out_specs=vmem_spec(),
        scratch_shapes=[VMEM((members, members), f32), VMEM((members, md), f32)],
        cost_estimate=pl.CostEstimate(
            flops=40_000_000, bytes_accessed=60_000_000, transcendentals=0
        ),
        name="solve",
    )(sums)

    mean_prior = jnp.sum(prior_all, 0, keepdims=True) / members
    anomaly = (prior_all - mean_prior) / spread_root
    change = lax.dot_general(
        gain, anomaly, (((0,), (0,)), ((), ())), precision=exact_mode, preferred_element_type=f32
    )
    posterior = prior_params + change.reshape(md, param_count, block_dev)
    return (posterior, predicted)


def solution(mesh):
    return jax.shard_map(
        shards,
        mesh=mesh,
        in_specs=(
            P("member", None, "basin"),
            P("member", None, "basin"),
            P("basin"),
            P("basin"),
            P("basin"),
            P("basin"),
            P("basin"),
            P(None, "basin"),
            P(None, "basin"),
            P("member", None, "basin"),
        ),
        out_specs=(P("member", None, "basin"), P("member", None, "basin")),
        check_vma=False,
    )
```

profile of v0, /device:TPU:0, one launch (start us, length us, event | category | flops | bytes accessed | tf_op | source)
XLA Modules:
  0.0 108.1 jit_solution(14687730031569749637)
XLA Ops:
  0.6 0.0 copy-start.3
  0.6 0.0 copy-start.4
  0.6 4.1 %collective-permute-start = (f32[1,32,8,128]{3,2,1,0:T(8,128)}, f32[1,32,8,128]{3,2,1,0:T(8,128)S(1)}, u32[]{:S(2)}, u32[]{:S(2)}) collective-permute-start(f32[1,32,8,128]{3,2,1,0:T(8,128)} %bitcast.69), channel_id=1, source_target_pairs={{0,16},{4,20},{8,24},{12,28},{16,0},{20,4},{24,8},{28,12},{1,17},{... | collective-permute-start | bytes 393224 | tf_op jit(solution)/shard_map/ppermute | solution.py:217
  4.8 1.0 copy.20
  5.8 0.7 convert_bitcast_fusion
  6.4 0.7 convert_bitcast_fusion.1
  7.1 1.8 %concatenate.18.x_ref = f32[72,128]{1,0:T(8,128)} concatenate(f32[32,128]{1,0:T(8,128)S(1)} %get-tuple-element.17, f32[32,128]{1,0:T(8,128)S(1)} %get-tuple-element.16, f32[1,128]{1,0:T(1,128)S(1)} %get-tuple-element.23, f32[1,128]{1,0:T(1,128)S(1)} %get-tuple-element.22, f32[4,128]{1,0:T(4,128)S(1)} %convert_bitcast_fusion, f32[2,128]{1,0:T(2,128)S(1)} %broadcast_in_dim.16), dimensions={0} | concatenate | bytes 73728 | tf_op jit(solution)/shard_map/concatenate | solution.py:449
  8.9 6.8 %exchange_1.1.meta_ref = f32[4,72,128]{2,1,0:T(8,128)} custom-call(f32[72,128]{1,0:T(8,128)} %concatenate.18.x_ref), custom_call_target="tpu_custom_call" | custom-call | tf_op jit(solution)/shard_map/exchange_1/pallas_call | solution.py:61
  15.8 0.7 slice_convert_fusion
  16.5 0.6 add_select_fusion
  17.1 1.1 %fusion.14 = (f32[32,1,512]{2,1,0:T(1,128)S(1)}, f32[32,1,512]{2,1,0:T(1,128)S(1)}) fusion(f32[32,2,512]{2,1,0:T(2,128)} %param.20), kind=kLoop, calls=%fused_computation.50 | loop fusion | bytes 262144 | tf_op jit(solution)/shard_map/slice | solution.py:516
  18.2 1.4 %slice_convert_fusion.1 = (s32[4,1,128]{2,1,0:T(1,128)}, s32[4,1,128]{2,1,0:T(1,128)}) fusion(f32[4,72,128]{2,1,0:T(8,128)} %exchange_1.1.meta_ref), kind=kLoop, calls=%fused_computation.45 | loop fusion | flops 1024 | bytes 8192 | tf_op jit(solution)/shard_map/convert_element_type | solution.py:462
  19.6 0.0 collective-permute-done
  19.6 0.9 pad_maximum_fusion.3
  20.5 1.6 %collective-permute-start.1 = (f32[2,32,8,128]{3,2,1,0:T(8,128)S(1)}, f32[2,32,8,128]{3,2,1,0:T(8,128)S(1)}, u32[]{:S(2)}, u32[]{:S(2)}) collective-permute-start(f32[2,32,8,128]{3,2,1,0:T(8,128)S(1)} %pad_maximum_fusion.3), channel_id=1, source_target_pairs={{0,8},{4,12},{8,0},{12,4},{16,24},{20,28},{24,16},{28,20},{1,9},{5... | collective-permute-start | bytes 786440 | tf_op jit(solution)/shard_map/ppermute | solution.py:217
  22.2 0.0 copy-done.3
  22.2 0.0 copy-done.4
  22.3 28.7 %route.1.x_ref = f32[4,64,512]{2,1,0:T(8,128)} custom-call(s32[1]{0:T(128)} %bitcast.basin_ref, s32[512]{0:T(512)} %bitcast.80, s32[512]{0:T(512)} %bitcast.79, s32[2048]{0:T(1024)} %get-tuple-element.19.gauge_row_ref, s32[2048]{0:T(1024)} %get-tuple-element.18.gauge_pack_ref, f32[4,72,128]{2,1,0:T(8,128)} %exchange_1.1.meta_ref, f32[32,8,128]{2,1,0:T(8,128)} %prior_ref.1, ...), custom_call_target="tpu_custom_call" | custom-call | flops 40000000 | bytes 60000000 | tf_op jit(solution)/shard_map/route/pallas_call | solution.py:481
  50.9 0.0 collective-permute-done.1
  51.0 0.1 collective-permute-start.2
  51.1 0.1 reduce_sum.31
  51.2 21.4 %observed_2.1 = f32[8,32,1024]{2,1,0:T(8,128)} custom-call(f32[4,64,512]{2,1,0:T(8,128)} %route.1.x_ref), custom_call_target="tpu_custom_call" | custom-call | tf_op jit(solution)/shard_map/observed_2/pallas_call | solution.py:143
  72.6 0.0 copy-start
  72.6 1.4 %reduce_sum.30 = f32[1024]{0:T(1024)S(1)} reduce(f32[8,32,1024]{2,1,0:T(8,128)} %observed_2.1, f32[]{:T(128)} %constant.56.clone.1), dimensions={0,1}, to_apply=%region_0.1 | reduce | flops 261120 | bytes 1052676 | tf_op jit(solution)/shard_map/reduce_sum | solution.py:518
  74.0 0.1 copy-done
  74.1 0.1 fusion.2
  74.3 0.1 pad_maximum_fusion
  74.4 0.1 subtract_divide_fusion
  74.6 0.0 slice-start
  74.6 1.9 %fusion.15.x_ref = f32[4,72,256]{2,1,0:T(8,128)} fusion(f32[4,72,1024]{2,1,0:T(8,128)S(1)} %bitcast.64, f32[256,1024,1]{1,0,2:T(8,128)S(1)} %bitcast.66), kind=kOutput, calls=%fused_computation.51 | convolution fusion | flops 905969664 | bytes 2523136 | tf_op jit(solution)/shard_map/dot_general | solution.py:523
  76.4 14.9 %sum_4.1 = f32[4,72,256]{2,1,0:T(8,128)} custom-call(f32[4,72,256]{2,1,0:T(8,128)} %fusion.15.x_ref), custom_call_target="tpu_custom_call" | custom-call | tf_op jit(solution)/shard_map/sum_4/pallas_call | solution.py:203
  91.4 0.0 slice-done
  91.4 0.8 reshape_squeeze.2
  92.2 12.7 %solve.1 = f32[256,32]{1,0:T(8,128)} custom-call(f32[288,256]{1,0:T(8,128)} %bitcast.71), custom_call_target="tpu_custom_call" | custom-call | flops 40000000 | bytes 60000000 | tf_op jit(solution)/shard_map/solve/pallas_call | solution.py:528
  104.8 0.0 collective-permute-done.2
  104.8 0.1 reduce_sum.32
  105.0 0.1 pad_maximum_fusion.1
  105.1 0.2 fusion.1
  105.3 0.0 copy-start.1
  105.3 0.0 copy-start.2
  105.3 0.3 copy.18
  105.7 0.5 copy-done.1
  106.2 0.1 copy-done.2
  106.3 1.1 %convolution_add_fusion = f32[32,8,128]{2,0,1:T(8,128)S(1)} fusion(f32[8,128,256]{2,1,0:T(8,128)S(1)} %bitcast.68, f32[256,32]{1,0:T(8,128)S(1)} %copy-done.2, f32[32,8,128]{2,1,0:T(8,128)S(1)} %copy-done.1), kind=kOutput, calls=%fused_computation.1 | convolution fusion | flops 100696064 | bytes 1343488 | tf_op jit(solution)/shard_map/dot_general | solution.py:542
  107.4 0.7 copy.21
  (11 shorter events, 0.1 us)
Async XLA Ops:
  0.6 21.5 %copy-start.3 = (f32[2,512]{1,0:T(2,128)S(1)}, f32[2,512]{1,0:T(2,128)}, u32[]{:S(2)}) copy-start(f32[2,512]{1,0:T(2,128)} %param.19) | copy-start | bytes 12292
  0.6 21.6 %copy-start.4 = (f32[2,512]{1,0:T(2,128)S(1)}, f32[2,512]{1,0:T(2,128)}, u32[]{:S(2)}) copy-start(f32[2,512]{1,0:T(2,128)} %param.18) | copy-start | bytes 12292
  0.6 19.0 %collective-permute-start = (f32[1,32,8,128]{3,2,1,0:T(8,128)}, f32[1,32,8,128]{3,2,1,0:T(8,128)S(1)}, u32[]{:S(2)}, u32[]{:S(2)}) collective-permute-start(f32[1,32,8,128]{3,2,1,0:T(8,128)} %bitcast.69), channel_id=1, source_target_pairs={{0,16},{4,20},{8,24},{12,28},{16,0},{20,4},{24,8},{28,12},{1,17},{... | collective-permute-start | bytes 393224 | tf_op jit(solution)/shard_map/ppermute | solution.py:217
  20.5 30.4 %collective-permute-start.1 = (f32[2,32,8,128]{3,2,1,0:T(8,128)S(1)}, f32[2,32,8,128]{3,2,1,0:T(8,128)S(1)}, u32[]{:S(2)}, u32[]{:S(2)}) collective-permute-start(f32[2,32,8,128]{3,2,1,0:T(8,128)S(1)} %pad_maximum_fusion.3), channel_id=1, source_target_pairs={{0,8},{4,12},{8,0},{12,4},{16,24},{20,28},{24,16},{28,20},{1,9},{5... | collective-permute-start | bytes 786440 | tf_op jit(solution)/shard_map/ppermute | solution.py:217
  51.0 53.9 %collective-permute-start.2 = (f32[4,32,8,128]{3,2,1,0:T(8,128)S(1)}, f32[4,32,8,128]{3,2,1,0:T(8,128)S(1)}, u32[]{:S(2)}, u32[]{:S(2)}) collective-permute-start(f32[4,32,8,128]{3,2,1,0:T(8,128)S(1)} %pad_maximum_fusion.2), channel_id=1, source_target_pairs={{0,4},{4,0},{8,12},{12,8},{16,20},{20,16},{24,28},{28,24},{1,5},{5... | collective-permute-start | bytes 1572872 | tf_op jit(solution)/shard_map/ppermute | solution.py:217
  72.6 1.5 %copy-start = (f32[8,32,1024]{2,1,0:T(8,128)S(1)}, f32[8,32,1024]{2,1,0:T(8,128)}, u32[]{:S(2)}) copy-start(f32[8,32,1024]{2,1,0:T(8,128)} %observed_2.1) | copy-start | bytes 3145732
  74.6 16.8 %slice-start = ((f32[8,32,1024]{2,1,0:T(8,128)}), f32[1,32,1024]{2,1,0:T(8,128)S(1)}, s32[]{:S(2)}) async-start(f32[8,32,1024]{2,1,0:T(8,128)} %observed_2.1), calls=%async_computation | async-start | bytes 262144 | tf_op jit(solution)/shard_map/slice | solution.py:510
  105.3 0.9 copy-start.1
  105.3 1.0 copy-start.2
where the time goes:
time: 109 us; the launch traced here: 108 us
  Pallas kernels  84.4 us (77%)
  other arithmetic  7.49 us (7%)
  local copies, waits for them, and re-layouts  6.49 us (6%)
  starting transfers between devices  5.84 us (5%)
  matrix products  2.97 us (3%)
    pallas_call x1, Pallas kernels, shards(): pl.pallas_call(functools.partial(route_body, basins, level_count, md, gau...  28.7 us
    pallas_call x1, Pallas kernels, observed_gather(): pl.pallas_call(functools.partial(observed_body, hours, n_basin, n), out_s...  21.4 us
    pallas_call x1, Pallas kernels, sum_over(): pl.pallas_call(functools.partial(sum_body, axis, n), out_shape=jax.ShapeD...  14.9 us
    pallas_call x1, Pallas kernels, shards(): pl.pallas_call(functools.partial(solve_body, n_member, md), out_shape=jax...  12.7 us
    pallas_call x1, Pallas kernels, exchange(): pl.pallas_call(functools.partial(exchange_body, axis, n, spread_out), out...  6.82 us
    ppermute x3, starting transfers between devices, permuted_step(): other = lax.ppermute(held, axis, [(i, i ^ bit) for i in range(n)])  5.84 us
    unnamed x15, local copies, waits for them, and re-layouts  2.47 us
  transfers between devices with their start and end apart: 3, of which 0 were waited for; matrix products, arithmetic and copies ran while one was open for 12% of the time, Pallas kernels for 78%

commit v1 on v0

--- a/solution.py
+++ b/solution.py
@@ -218,12 +218,18 @@
     return jnp.concatenate([held, other], 0)
 
 
+def split_two(values):
+    high = values.astype(jnp.bfloat16)
+    low = (values - high.astype(jnp.float32)).astype(jnp.bfloat16)
+    return jnp.concatenate([high, low], axis=1)
+
+
 def route_body(
     seg_count, level_count, members, gauges, hours, param_count,
-    basin_ref, down_ref, count_ref, gauge_row_ref, gauge_pack_ref,
-    meta_ref, prior_ref, cos_ref, pin_ref, pout_ref, lat_hbm,
+    basin_ref, meta_ref, prior_ref, cos_ref, pin_ref, pout_ref, lat_hbm,
     out_ref,
-    up_ref, flow_ref, row_ref, now_ref, back_ref, carry_ref, par_ref, raw_ref, ready_ref, sem,
+    up_ref, flow_ref, row_ref, now_ref, back_ref, carry_ref, par_ref, raw_ref, ready_ref,
+    int_ref, table_ref, sem, table_sem,
 ):
     first = basin_ref[0]
     lev = BLK_LEV
@@ -245,11 +251,24 @@
         for m in range(members):
             fetch(c, m).start()
 
+    tile = int_ref.shape[1]
+    tile_sub = lax.broadcasted_iota(jnp.int32, (tile, LANES), 0)
+
+    def integers(seg, _):
+        value = meta_ref[seg, 2 * members :, :].astype(jnp.int32)
+        row = value // LANES * (hours * members) + value % members
+        int_ref[seg] = jnp.where(tile_sub < 2, value, row)
+        return 0
+
+    lax.fori_loop(first, seg_count, integers, 0)
+    table = pltpu.make_async_copy(int_ref, table_ref, table_sem)
+    table.start()
+
     def clear(i, _):
         up_ref[i] = jnp.zeros((2 * rows, LANES), jnp.float32)
         return 0
 
-    lax.fori_loop(0, 2 * lev, clear, 0, unroll=8)
+    lax.fori_loop(lev, 2 * lev, clear, 0, unroll=8)
 
     def turned(values):
         return jnp.concatenate([values] * packs, axis=0).T
@@ -268,30 +287,35 @@
     for k in range(param_count - 2):
         par_ref[k] = turned(0.2 * prior_ref[:, 2 + k, :])
 
-    def place_group(tiles):
-        flat = jnp.concatenate(tiles, axis=0).T
+    group_of = lane // members
+    row_group = lax.broadcasted_iota(jnp.int32, (1, LANES), 1) // members
+
+    def pick(pieces, order, where):
+        made = pieces[order(0)]
+        for q in range(1, packs):
+            made = jnp.where(where == q, pieces[order(q)], made)
+        return made
+
+    def place_group(tiles, where):
+        mixed = [pick(tiles, lambda q, g=g: (g - q) % packs, where) for g in range(packs)]
+        mixed = [jnp.broadcast_to(tile, shape) for tile in mixed]
+        flat = jnp.concatenate(mixed, axis=0).T
         strips = [flat[q * rows : (q + 1) * rows] for q in range(packs)]
         made = []
         for i in range(packs):
-            total = None
-            for q in range(packs):
-                shift = ((q - i) * members) % LANES
-                piece = pltpu.roll(strips[q], shift, 1) if shift else strips[q]
-                total = piece if total is None else jnp.where(lane // members == q, piece, total)
-            made.append(total)
+            turn = pick(strips, lambda g, i=i: (g - i) % packs, group_of)
+            made.append(pltpu.roll(turn, LANES - i * members, 1) if i else turn)
         return made
 
     def relayout(group, _):
         base = group * packs
         for h in range(hours):
             tiles = [raw_ref[(base + i) * hours + h] for i in range(packs)]
-            for i, tile in enumerate(place_group(tiles)):
+            for i, tile in enumerate(place_group(tiles, group_of)):
                 ready_ref[base + i, h] = tile
         for n, ref in enumerate((pin_ref, pout_ref)):
-            tiles = [
-                jnp.broadcast_to(ref[pl.ds(base + i, 1), :], shape) for i in range(packs)
-            ]
-            for i, tile in enumerate(place_group(tiles)):
+            tiles = [ref[pl.ds(base + i, 1), :] for i in range(packs)]
+            for i, tile in enumerate(place_group(tiles, row_group)):
                 ready_ref[base + i, hours + n] = tile
         return 0
 
@@ -299,13 +323,15 @@
     for c in range(chunks):
         for m in range(members):
             fetch(c, m).wait()
-        lax.fori_loop(c * chunk_groups, (c + 1) * chunk_groups, relayout, 0, unroll=2)
+        lax.fori_loop(c * chunk_groups, (c + 1) * chunk_groups, relayout, 0, unroll=4)
+
+    table.wait()
 
     def sweep(seg, level, parity, own):
         def block(j, _):
             here = level * lev + j
             b = seg * seg_blocks + here
-            live = place < count_ref[b]
+            live = place < table_ref[seg, 1, here]
             now = now_ref[pl.ds(b, 1), :]
             back = back_ref[pl.ds(b, 1), :]
             carry = carry_ref[pl.ds(b, 1), :]
@@ -331,35 +357,29 @@
             up_ref[parity * lev + j] = jnp.zeros((2 * rows, LANES), jnp.float32)
             flow_ref[pl.ds(here * 2 * rows, rows), :] = out0
             flow_ref[pl.ds(here * 2 * rows + rows, rows), :] = out1
-            target = (1 - parity) * lev + down_ref[b]
+            target = (1 - parity) * lev + table_ref[seg, 0, here]
             up_ref[target, :rows] += out0
             up_ref[target, rows:] += out1
             return 0
 
         lax.fori_loop(0, lev, block, 0, unroll=4)
 
-    fold = lax.broadcasted_iota(jnp.int32, shape, 0) == lane % members
-    fold = fold.astype(jnp.float32)
-    one_lane = lax.broadcasted_iota(jnp.int32, (1, LANES), 1) // members
-
     def observe(seg):
-        first_gauge = seg * gauges
-
-        def one(g, _):
-            row = gauge_row_ref[first_gauge + g]
-            keep = one_lane == gauge_pack_ref[first_gauge + g]
-            row_ref[pl.ds(g, 1), :] = jnp.where(keep, flow_ref[pl.ds(row, 1), :], 0.0)
-            row_ref[pl.ds(gauges + g, 1), :] = jnp.where(
-                keep, flow_ref[pl.ds(row + rows, 1), :], 0.0
-            )
+        def part_of(part, _):
+            for g in range(LANES):
+                row = table_ref[seg, 2 + part, g]
+                row_ref[0, g : g + 1, :] = flow_ref[pl.ds(row, 1), :]
+                row_ref[1, g : g + 1, :] = flow_ref[pl.ds(row + rows, 1), :]
+            slot = meta_ref[seg, pl.ds(2 * members + 2 + part, 1), :].astype(jnp.int32)
+            pack = slot % LANES // members
+            span = pl.ds(pl.multiple_of(part * LANES, LANES), LANES)
+            for h in range(hours):
+                turned_rows = row_ref[h].T
+                strips = [turned_rows[q * rows : (q + 1) * rows] for q in range(packs)]
+                out_ref[seg, h * members : (h + 1) * members, span] = pick(strips, lambda q: q, pack)
             return 0
 
-        lax.fori_loop(0, gauges, one, 0, unroll=8)
-        for h in range(2):
-            out_ref[seg, h * members : (h + 1) * members, :] = lax.dot_general(
-                fold, row_ref[h * gauges : (h + 1) * gauges, :], (((1,), (1,)), ((), ())),
-                precision=exact_mode, preferred_element_type=jnp.float32,
-            )
+        lax.fori_loop(0, gauges // LANES, part_of, 0)
 
     def nothing(seg, _):
         out_ref[seg] = jnp.zeros(out_ref.shape[1:], jnp.float32)
@@ -458,11 +478,6 @@
         0,
     )
     meta_all = exchange(meta, "basin", 1)
-    down_all = meta_all[:, md * 2].reshape(-1).astype(jnp.int32)
-    count_all = meta_all[:, md * 2 + 1].reshape(-1).astype(jnp.int32)
-    slots = meta_all[:, md * 2 + 2 : md * 2 + 2 + gauge_rows].reshape(-1).astype(jnp.int32)
-    gauge_row = slots // LANES * (hours * md) + slots % md
-    gauge_pack = slots % LANES // md
 
     modes = param_count - 2
     lane_pos = np.arange(LANES)
@@ -481,26 +496,29 @@
     parts = pl.pallas_call(
         functools.partial(route_body, basins, level_count, md, gauges, hours, param_count),
         out_shape=jax.ShapeDtypeStruct((basins, 2 * md, gauges), f32),
-        in_specs=[smem_spec()] * 5 + [vmem_spec()] * 5 + [pl.BlockSpec(memory_space=pl.ANY)],
+        in_specs=[smem_spec()] + [vmem_spec()] * 5 + [pl.BlockSpec(memory_space=pl.ANY)],
         out_specs=vmem_spec(),
         scratch_shapes=[
             VMEM((2 * BLK_LEV, 2 * md, LANES), f32),
             VMEM((block_dev * 2 * md, LANES), f32),
-            VMEM((2 * gauges, LANES), f32),
+            VMEM((hours, LANES, LANES), f32),
             seg_coef,
             seg_coef,
             seg_coef,
             VMEM((modes, block_dev, LANES), f32),
             VMEM((block_dev * hours, md, LANES), f32),
             VMEM((block_dev, hours + 2, md, LANES), f32),
+            VMEM((basins, meta.shape[0] - 2 * md, LANES), jnp.int32),
+            SMEM((basins, meta.shape[0] - 2 * md, LANES), jnp.int32),
             pltpu.SemaphoreType.DMA((4, md)),
+            pltpu.SemaphoreType.DMA,
         ],
         cost_estimate=pl.CostEstimate(
             flops=40_000_000, bytes_accessed=60_000_000, transcendentals=0
         ),
         name="route",
     )(
-        basin_idx, down_all, count_all, gauge_row, gauge_pack, meta_all, prior_params, cosine,
+        basin_idx, meta_all, prior_params, cosine,
         inflow_start.reshape(block_dev, LANES), outflow_start.reshape(block_dev, LANES), lateral,
     )
     parts, held = lax.optimization_barrier((parts, held))

time: 109 us -> 97.7 us (0.90)
  Pallas kernels: 84.4 us -> 76.2 us
  other arithmetic: 7.49 us -> 4.75 us
    pallas_call x1, Pallas kernels: 28.7 us -> 20.3 us  [shards(): pl.pallas_call(functools.partial(route_body, basins, level_count, md, gau...]
    convert_element_type x2 -> x0, other arithmetic: 2.12 us -> none  [the longest x1 1.4 us: shards(): count_all = meta_all[:, md * 2 + 1].reshape(-1).astype(jnp.int32)]
  transfers between devices with their start and end apart: 3 -> 3, of which waited for: 0 -> 0; matrix products, arithmetic and copies ran while one was open for 12% -> 10% of each run, Pallas kernels for 78% -> 78%
where the time goes in v1:
time: 97.7 us; the launch traced here: 97.1 us
  Pallas kernels  76.2 us (78%)
  local copies, waits for them, and re-layouts  6.5 us (7%)
  starting transfers between devices  5.84 us (6%)
  other arithmetic  4.75 us (5%)
  matrix products  2.97 us (3%)
    pallas_call x1, Pallas kernels, observed_gather(): pl.pallas_call(functools.partial(observed_body, hours, n_basin, n), out_s...  21.4 us
    pallas_call x1, Pallas kernels, shards(): pl.pallas_call(functools.partial(route_body, basins, level_count, md, gau...  20.3 us
    pallas_call x1, Pallas kernels, sum_over(): pl.pallas_call(functools.partial(sum_body, axis, n), out_shape=jax.ShapeD...  14.9 us
    pallas_call x1, Pallas kernels, shards(): pl.pallas_call(functools.partial(solve_body, n_member, md), out_shape=jax...  12.7 us
    pallas_call x1, Pallas kernels, exchange(): pl.pallas_call(functools.partial(exchange_body, axis, n, spread_out), out...  6.82 us
    ppermute x3, starting transfers between devices, permuted_step(): other = lax.ppermute(held, axis, [(i, i ^ bit) for i in range(n)])  5.84 us
    unnamed x15, local copies, waits for them, and re-layouts  2.47 us
  transfers between devices with their start and end apart: 3, of which 0 were waited for; matrix products, arithmetic and copies ran while one was open for 10% of the time, Pallas kernels for 78%

profile of v1, /device:TPU:0, one launch (start us, length us, event | category | flops | bytes accessed | tf_op | source)
XLA Modules:
  0.0 97.1 jit_solution(17230641704362834428)
XLA Ops:
  0.6 0.0 copy-start.3
  0.6 0.0 copy-start.4
  0.6 4.1 %collective-permute-start = (f32[1,32,8,128]{3,2,1,0:T(8,128)}, f32[1,32,8,128]{3,2,1,0:T(8,128)S(1)}, u32[]{:S(2)}, u32[]{:S(2)}) collective-permute-start(f32[1,32,8,128]{3,2,1,0:T(8,128)} %bitcast.66), channel_id=1, source_target_pairs={{0,16},{4,20},{8,24},{12,28},{16,0},{20,4},{24,8},{28,12},{1,17},{... | collective-permute-start | bytes 393224 | tf_op jit(solution)/shard_map/ppermute | solution.py:217
  4.8 1.0 copy.20
  5.8 0.7 convert_bitcast_fusion
  6.4 0.7 convert_bitcast_fusion.1
  7.1 1.8 %concatenate.19.x_ref = f32[72,128]{1,0:T(8,128)} concatenate(f32[32,128]{1,0:T(8,128)S(1)} %get-tuple-element.15, f32[32,128]{1,0:T(8,128)S(1)} %get-tuple-element.14, f32[1,128]{1,0:T(1,128)S(1)} %get-tuple-element.19, f32[1,128]{1,0:T(1,128)S(1)} %get-tuple-element.18, f32[4,128]{1,0:T(4,128)S(1)} %convert_bitcast_fusion, f32[2,128]{1,0:T(2,128)S(1)} %broadcast_in_dim.17), dimensions={0} | concatenate | bytes 73728 | tf_op jit(solution)/shard_map/concatenate | solution.py:469
  8.9 6.8 %exchange_1.1.meta_ref = f32[4,72,128]{2,1,0:T(8,128)} custom-call(f32[72,128]{1,0:T(8,128)} %concatenate.19.x_ref), custom_call_target="tpu_custom_call" | custom-call | tf_op jit(solution)/shard_map/exchange_1/pallas_call | solution.py:61
  15.8 1.1 %fusion.7 = (f32[32,1,512]{2,1,0:T(1,128)S(1)}, f32[32,1,512]{2,1,0:T(1,128)S(1)}) fusion(f32[32,2,512]{2,1,0:T(2,128)} %param.20), kind=kLoop, calls=%fused_computation.27 | loop fusion | bytes 262144 | tf_op jit(solution)/shard_map/slice | solution.py:534
  16.9 0.0 collective-permute-done
  16.9 0.9 pad_maximum_fusion.3
  17.8 1.6 %collective-permute-start.1 = (f32[2,32,8,128]{3,2,1,0:T(8,128)S(1)}, f32[2,32,8,128]{3,2,1,0:T(8,128)S(1)}, u32[]{:S(2)}, u32[]{:S(2)}) collective-permute-start(f32[2,32,8,128]{3,2,1,0:T(8,128)S(1)} %pad_maximum_fusion.3), channel_id=1, source_target_pairs={{0,8},{4,12},{8,0},{12,4},{16,24},{20,28},{24,16},{28,20},{1,9},{5... | collective-permute-start | bytes 786440 | tf_op jit(solution)/shard_map/ppermute | solution.py:217
  19.5 0.0 copy-done.3
  19.5 0.0 copy-done.4
  19.5 20.3 %route.1.x_ref = f32[4,64,512]{2,1,0:T(8,128)} custom-call(s32[1]{0:T(128)} %bitcast.basin_ref, f32[4,72,128]{2,1,0:T(8,128)} %exchange_1.1.meta_ref, f32[32,8,128]{2,1,0:T(8,128)} %prior_ref.1, f32[6,32,128]{2,1,0:T(8,128)} %constant.21.clone.cos_ref, f32[128,128]{1,0:T(8,128)} %bitcast.69, f32[128,128]{1,0:T(8,128)} %bitcast.70, f32[32,256,128]{2,1,0:T(8,128)} %bitcast.62), custom_call_target="tpu_custom_call" | custom-call | flops 40000000 | bytes 60000000 | tf_op jit(solution)/shard_map/route/pallas_call | solution.py:496
  39.9 0.0 collective-permute-done.1
  39.9 0.1 collective-permute-start.2
  40.0 0.1 reduce_sum.31
  40.2 21.4 %observed_2.1 = f32[8,32,1024]{2,1,0:T(8,128)} custom-call(f32[4,64,512]{2,1,0:T(8,128)} %route.1.x_ref), custom_call_target="tpu_custom_call" | custom-call | tf_op jit(solution)/shard_map/observed_2/pallas_call | solution.py:143
  61.5 0.0 copy-start
  61.6 1.4 %reduce_sum.30 = f32[1024]{0:T(1024)S(1)} reduce(f32[8,32,1024]{2,1,0:T(8,128)} %observed_2.1, f32[]{:T(128)} %constant.8.clone.1), dimensions={0,1}, to_apply=%region_0.0 | reduce | flops 261120 | bytes 1052676 | tf_op jit(solution)/shard_map/reduce_sum | solution.py:536
  63.0 0.1 copy-done
  63.1 0.1 fusion.2
  63.3 0.1 pad_maximum_fusion
  63.4 0.1 subtract_divide_fusion
  63.5 0.0 slice-start
  63.6 1.9 %fusion.8.x_ref = f32[4,72,256]{2,1,0:T(8,128)} fusion(f32[4,72,1024]{2,1,0:T(8,128)S(1)} %bitcast.61, f32[256,1024,1]{1,0,2:T(8,128)S(1)} %bitcast.63), kind=kOutput, calls=%fused_computation.28 | convolution fusion | flops 905969664 | bytes 2523136 | tf_op jit(solution)/shard_map/dot_general | solution.py:541
  65.4 14.9 %sum_4.1 = f32[4,72,256]{2,1,0:T(8,128)} custom-call(f32[4,72,256]{2,1,0:T(8,128)} %fusion.8.x_ref), custom_call_target="tpu_custom_call" | custom-call | tf_op jit(solution)/shard_map/sum_4/pallas_call | solution.py:203
  80.4 0.0 slice-done
  80.4 0.8 reshape_squeeze.3
  81.1 12.7 %solve.1 = f32[256,32]{1,0:T(8,128)} custom-call(f32[288,256]{1,0:T(8,128)} %bitcast.68), custom_call_target="tpu_custom_call" | custom-call | flops 40000000 | bytes 60000000 | tf_op jit(solution)/shard_map/solve/pallas_call | solution.py:546
  93.8 0.0 collective-permute-done.2
  93.8 0.1 reduce_sum.32
  94.0 0.1 pad_maximum_fusion.1
  94.0 0.2 fusion.1
  94.3 0.0 copy-start.1
  94.3 0.0 copy-start.2
  94.3 0.3 copy.18
  94.7 0.5 copy-done.1
  95.2 0.1 copy-done.2
  95.3 1.1 %convolution_add_fusion = f32[32,8,128]{2,0,1:T(8,128)S(1)} fusion(f32[8,128,256]{2,1,0:T(8,128)S(1)} %bitcast.65, f32[256,32]{1,0:T(8,128)S(1)} %copy-done.2, f32[32,8,128]{2,1,0:T(8,128)S(1)} %copy-done.1), kind=kOutput, calls=%fused_computation.1 | convolution fusion | flops 100696064 | bytes 1343488 | tf_op jit(solution)/shard_map/dot_general | solution.py:560
  96.4 0.7 copy.21
  (11 shorter events, 0.1 us)
Async XLA Ops:
  0.6 18.8 %copy-start.3 = (f32[2,512]{1,0:T(2,128)S(1)}, f32[2,512]{1,0:T(2,128)}, u32[]{:S(2)}) copy-start(f32[2,512]{1,0:T(2,128)} %param.19) | copy-start | bytes 12292
  0.6 18.9 %copy-start.4 = (f32[2,512]{1,0:T(2,128)S(1)}, f32[2,512]{1,0:T(2,128)}, u32[]{:S(2)}) copy-start(f32[2,512]{1,0:T(2,128)} %param.18) | copy-start | bytes 12292
  0.6 16.2 %collective-permute-start = (f32[1,32,8,128]{3,2,1,0:T(8,128)}, f32[1,32,8,128]{3,2,1,0:T(8,128)S(1)}, u32[]{:S(2)}, u32[]{:S(2)}) collective-permute-start(f32[1,32,8,128]{3,2,1,0:T(8,128)} %bitcast.66), channel_id=1, source_target_pairs={{0,16},{4,20},{8,24},{12,28},{16,0},{20,4},{24,8},{28,12},{1,17},{... | collective-permute-start | bytes 393224 | tf_op jit(solution)/shard_map/ppermute | solution.py:217
  17.8 22.1 %collective-permute-start.1 = (f32[2,32,8,128]{3,2,1,0:T(8,128)S(1)}, f32[2,32,8,128]{3,2,1,0:T(8,128)S(1)}, u32[]{:S(2)}, u32[]{:S(2)}) collective-permute-start(f32[2,32,8,128]{3,2,1,0:T(8,128)S(1)} %pad_maximum_fusion.3), channel_id=1, source_target_pairs={{0,8},{4,12},{8,0},{12,4},{16,24},{20,28},{24,16},{28,20},{1,9},{5... | collective-permute-start | bytes 786440 | tf_op jit(solution)/shard_map/ppermute | solution.py:217
  39.9 53.9 %collective-permute-start.2 = (f32[4,32,8,128]{3,2,1,0:T(8,128)S(1)}, f32[4,32,8,128]{3,2,1,0:T(8,128)S(1)}, u32[]{:S(2)}, u32[]{:S(2)}) collective-permute-start(f32[4,32,8,128]{3,2,1,0:T(8,128)S(1)} %pad_maximum_fusion.2), channel_id=1, source_target_pairs={{0,4},{4,0},{8,12},{12,8},{16,20},{20,16},{24,28},{28,24},{1,5},{5... | collective-permute-start | bytes 1572872 | tf_op jit(solution)/shard_map/ppermute | solution.py:217
  61.5 1.5 %copy-start = (f32[8,32,1024]{2,1,0:T(8,128)S(1)}, f32[8,32,1024]{2,1,0:T(8,128)}, u32[]{:S(2)}) copy-start(f32[8,32,1024]{2,1,0:T(8,128)} %observed_2.1) | copy-start | bytes 3145732
  63.5 16.8 %slice-start = ((f32[8,32,1024]{2,1,0:T(8,128)}), f32[1,32,1024]{2,1,0:T(8,128)S(1)}, s32[]{:S(2)}) async-start(f32[8,32,1024]{2,1,0:T(8,128)} %observed_2.1), calls=%async_computation | async-start | bytes 262144 | tf_op jit(solution)/shard_map/slice | solution.py:528
  94.3 0.9 copy-start.1
  94.3 1.0 copy-start.2

commit v2 on v1

--- a/solution.py
+++ b/solution.py
@@ -25,52 +25,77 @@
     return pl.BlockSpec(memory_space=SMEM)
 
 
-def exchange_body(axis, n, spread_out, x_ref, o_ref, send_sem, recv_sem, own_sem):
-    me = lax.axis_index(axis)
+def exchange_body(
+    n, prior_ref, down_ref, count_ref, gauge_ref, coef_ref, table_ref, send_sem, recv_sem, own_sem
+):
+    me = lax.axis_index("basin")
     barrier = pltpu.get_barrier_semaphore()
     for i in range(1, n):
-        pl.semaphore_signal(
-            barrier, inc=1, device_id={axis: lax.rem(me + i, n)}, device_id_type=MESH
+        @pl.when(me + i < n)
+        def _():
+            pl.semaphore_signal(
+                barrier, inc=1, device_id={"basin": lax.rem(me + i, n)}, device_id_type=MESH
+            )
+    @pl.when(me > 0)
+    def _():
+        pl.semaphore_wait(barrier, me)
+
+    gauge_rows = gauge_ref.shape[0]
+    pieces = [
+        (prior_ref.at[:, 0:2, :], coef_ref.at[me, :, 0:2, :]),
+        (down_ref, table_ref.at[me, 0:1, :]),
+        (count_ref, table_ref.at[me, 1:2, :]),
+        (gauge_ref, table_ref.at[me, 2 : 2 + gauge_rows, :]),
+    ]
+
+    def remote(i, k):
+        src, dst = pieces[k]
+        return pltpu.make_async_remote_copy(
+            src_ref=src, dst_ref=dst,
+            send_sem=send_sem.at[i - 1, k], recv_sem=recv_sem.at[i - 1, k],
+            device_id={"basin": lax.rem(me - i + n, n)}, device_id_type=MESH,
         )
-    pl.semaphore_wait(barrier, n - 1)
-    copies = []
+
     for i in range(1, n):
-        peer = lax.rem(me + i, n)
-        copies.append(
-            pltpu.make_async_remote_copy(
-                src_ref=x_ref.at[peer] if spread_out else x_ref,
-                dst_ref=o_ref.at[me],
-                send_sem=send_sem.at[i - 1],
-                recv_sem=recv_sem.at[i - 1],
-                device_id={axis: peer},
-                device_id_type=MESH,
-            )
-        )
-    for copy in copies:
+        @pl.when(me - i >= 0)
+        def _():
+            for k in range(len(pieces)):
+                remote(i, k).start()
+    own = [pltpu.make_async_copy(src, dst, own_sem.at[k]) for k, (src, dst) in enumerate(pieces)]
+    for copy in own:
         copy.start()
-    own = pltpu.make_async_copy(x_ref.at[me] if spread_out else x_ref, o_ref.at[me], own_sem)
-    own.start()
-    own.wait()
-    for copy in copies:
+    for copy in own:
         copy.wait()
-
-
-def exchange(x, axis, collective_id, spread_out=False):
-    n = lax.axis_size(axis)
-    shape = x.shape if spread_out else (n,) + x.shape
+    for i in range(1, n):
+        @pl.when(me + i < n)
+        def _():
+            for k in range(len(pieces)):
+                remote(i, k).wait_recv()
+
+        @pl.when(me - i >= 0)
+        def _():
+            for k in range(len(pieces)):
+                remote(i, k).wait_send()
+
+
+def exchange(prior, down, count, gauge, collective_id):
+    n = lax.axis_size("basin")
     return pl.pallas_call(
-        functools.partial(exchange_body, axis, n, spread_out),
-        out_shape=jax.ShapeDtypeStruct(shape, x.dtype),
-        in_specs=[vmem_spec()],
-        out_specs=vmem_spec(),
+        functools.partial(exchange_body, n),
+        out_shape=(
+            jax.ShapeDtypeStruct((n,) + prior.shape, prior.dtype),
+            jax.ShapeDtypeStruct((n, 8, LANES), down.dtype),
+        ),
+        in_specs=[vmem_spec()] * 4,
+        out_specs=(vmem_spec(), vmem_spec()),
         scratch_shapes=[
-            pltpu.SemaphoreType.DMA((n - 1,)),
-            pltpu.SemaphoreType.DMA((n - 1,)),
-            pltpu.SemaphoreType.DMA,
+            pltpu.SemaphoreType.DMA((n - 1, 4)),
+            pltpu.SemaphoreType.DMA((n - 1, 4)),
+            pltpu.SemaphoreType.DMA((4,)),
         ],
         compiler_params=pltpu.CompilerParams(collective_id=collective_id, has_side_effects=True),
         name=f"exchange_{collective_id}",
-    )(x)
+    )(prior, down, count, gauge)
 
 
 def doubling_bits(n):
@@ -226,7 +251,7 @@
 
 def route_body(
     seg_count, level_count, members, gauges, hours, param_count,
-    basin_ref, meta_ref, prior_ref, cos_ref, pin_ref, pout_ref, lat_hbm,
+    basin_ref, coef_ref, given_ref, prior_ref, cos_ref, pin_ref, pout_ref, lat_hbm,
     out_ref,
     up_ref, flow_ref, row_ref, now_ref, back_ref, carry_ref, par_ref, raw_ref, ready_ref,
     int_ref, table_ref, sem, table_sem,
@@ -255,7 +280,7 @@
     tile_sub = lax.broadcasted_iota(jnp.int32, (tile, LANES), 0)
 
     def integers(seg, _):
-        value = meta_ref[seg, 2 * members :, :].astype(jnp.int32)
+        value = given_ref[seg]
         row = value // LANES * (hours * members) + value % members
         int_ref[seg] = jnp.where(tile_sub < 2, value, row)
         return 0
@@ -274,8 +299,8 @@
         return jnp.concatenate([values] * packs, axis=0).T
 
     def coefficients(seg, _):
-        storage = 0.02 + 0.1 * jax.nn.sigmoid(meta_ref[seg, :members, :])
-        weighting = 0.2 * jax.nn.sigmoid(meta_ref[seg, members : 2 * members, :])
+        storage = 0.02 + 0.1 * jax.nn.sigmoid(coef_ref[seg, :, 0, :])
+        weighting = 0.2 * jax.nn.sigmoid(coef_ref[seg, :, 1, :])
         den = storage * (1.0 - weighting) + 0.5
         span = pl.ds(pl.multiple_of(seg * seg_blocks, seg_blocks), seg_blocks)
         now_ref[span, :] = turned((0.5 - storage * weighting) / den)
@@ -370,7 +395,7 @@
                 row = table_ref[seg, 2 + part, g]
                 row_ref[0, g : g + 1, :] = flow_ref[pl.ds(row, 1), :]
                 row_ref[1, g : g + 1, :] = flow_ref[pl.ds(row + rows, 1), :]
-            slot = meta_ref[seg, pl.ds(2 * members + 2 + part, 1), :].astype(jnp.int32)
+            slot = given_ref[seg, pl.ds(2 + part, 1), :]
             pack = slot % LANES // members
             span = pl.ds(pl.multiple_of(part * LANES, LANES), LANES)
             for h in range(hours):
@@ -464,20 +489,10 @@
     prior_steps = doubling_bits(n_member)
     held = permuted_step(prior_params[None], "member", prior_steps[0])
 
-    gauge_rows = gauges // block_dev
-    extra = -(md * 2 + 2 + gauge_rows) % 8
-    meta = jnp.concatenate(
-        [
-            prior_params[:, 0, :],
-            prior_params[:, 1, :],
-            downstream.astype(f32)[None],
-            reach_count.astype(f32)[None],
-            gauge_reach.astype(f32).reshape(-1, block_dev),
-            jnp.zeros((extra, block_dev), f32),
-        ],
-        0,
+    coef_all, table_all = exchange(
+        prior_params, downstream.reshape(1, block_dev), reach_count.reshape(1, block_dev),
+        gauge_reach.reshape(-1, block_dev), 1,
     )
-    meta_all = exchange(meta, "basin", 1)
 
     modes = param_count - 2
     lane_pos = np.arange(LANES)
@@ -487,7 +502,7 @@
 
     lateral = lateral_flow.reshape(md, hours, block_dev, LANES)
     lateral = jnp.swapaxes(lateral, 1, 2).reshape(md, block_dev * hours, LANES)
-    held, meta_all = lax.optimization_barrier((held, meta_all))
+    held, coef_all = lax.optimization_barrier((held, coef_all))
     for bit in prior_steps[1:-1]:
         held = permuted_step(held, "member", bit)
     basin_idx = lax.axis_index("basin").astype(jnp.int32).reshape(1)
@@ -496,7 +511,7 @@
     parts = pl.pallas_call(
         functools.partial(route_body, basins, level_count, md, gauges, hours, param_count),
         out_shape=jax.ShapeDtypeStruct((basins, 2 * md, gauges), f32),
-        in_specs=[smem_spec()] + [vmem_spec()] * 5 + [pl.BlockSpec(memory_space=pl.ANY)],
+        in_specs=[smem_spec()] + [vmem_spec()] * 6 + [pl.BlockSpec(memory_space=pl.ANY)],
         out_specs=vmem_spec(),
         scratch_shapes=[
             VMEM((2 * BLK_LEV, 2 * md, LANES), f32),
@@ -508,8 +523,8 @@
             VMEM((modes, block_dev, LANES), f32),
             VMEM((block_dev * hours, md, LANES), f32),
             VMEM((block_dev, hours + 2, md, LANES), f32),
-            VMEM((basins, meta.shape[0] - 2 * md, LANES), jnp.int32),
-            SMEM((basins, meta.shape[0] - 2 * md, LANES), jnp.int32),
+            VMEM(table_all.shape, jnp.int32),
+            SMEM(table_all.shape, jnp.int32),
             pltpu.SemaphoreType.DMA((4, md)),
             pltpu.SemaphoreType.DMA,
         ],
@@ -518,7 +533,7 @@
         ),
         name="route",
     )(
-        basin_idx, meta_all, prior_params, cosine,
+        basin_idx, coef_all, table_all, prior_params, cosine,
         inflow_start.reshape(block_dev, LANES), outflow_start.reshape(block_dev, LANES), lateral,
     )
     parts, held = lax.optimization_barrier((parts, held))

time: 97.7 us -> 92.1 us (0.943)
  Pallas kernels: 76.2 us -> 73.2 us
  local copies, waits for them, and re-layouts: 6.5 us -> 4.26 us
    pallas_call x1, Pallas kernels: 21.4 us -> 19.4 us  [observed_gather(): pl.pallas_call(functools.partial(observed_body, hours, n_basin, n), out_s...]
    concatenate x1 -> x0, local copies, waits for them, and re-layouts: 1.82 us -> none  [shards(): jnp.concatenate([prior_params[:, 0, :], prior_params[:, 1, :], downstream...]
    pallas_call x1, Pallas kernels: 14.9 us -> 13.1 us  [sum_over(): pl.pallas_call(functools.partial(sum_body, axis, n), out_shape=jax.ShapeD...]
    unnamed x15 -> x10, local copies, waits for them, and re-layouts: 2.47 us -> 2.05 us
  transfers between devices with their start and end apart: 3 -> 3, of which waited for: 0 -> 0; matrix products, arithmetic and copies ran while one was open for 10% -> 8% of each run, Pallas kernels for 78% -> 59%
where the time goes in v2:
time: 92.1 us; the launch traced here: 91.5 us
  Pallas kernels  73.2 us (79%)
  starting transfers between devices  6.21 us (7%)
  local copies, waits for them, and re-layouts  4.26 us (5%)
  other arithmetic  3.98 us (4%)
  matrix products  2.96 us (3%)
    pallas_call x1, Pallas kernels, shards(): pl.pallas_call(functools.partial(route_body, basins, level_count, md, gau...  20.6 us
    pallas_call x1, Pallas kernels, observed_gather(): pl.pallas_call(functools.partial(observed_body, hours, n_basin, n), out_s...  19.4 us
    pallas_call x1, Pallas kernels, sum_over(): pl.pallas_call(functools.partial(sum_body, axis, n), out_shape=jax.ShapeD...  13.1 us
    pallas_call x1, Pallas kernels, shards(): pl.pallas_call(functools.partial(solve_body, n_member, md), out_shape=jax...  12.7 us
    pallas_call x1, Pallas kernels, exchange(): pl.pallas_call(functools.partial(exchange_body, n), out_shape=(jax.ShapeD...  7.34 us
    ppermute x3, starting transfers between devices, permuted_step(): other = lax.ppermute(held, axis, [(i, i ^ bit) for i in range(n)])  6.21 us
    unnamed x10, local copies, waits for them, and re-layouts  2.05 us
    dot_general x1, matrix products, shards(): lax.dot_general(both, scaled_all, (((1,), (1,)), ((), ())), precision=exa...  1.85 us
  transfers between devices with their start and end apart: 3, of which 0 were waited for; matrix products, arithmetic and copies ran while one was open for 8% of the time, Pallas kernels for 59%

profile of v2, /device:TPU:0, one launch (start us, length us, event | category | flops | bytes accessed | tf_op | source)
XLA Modules:
  0.0 91.5 jit_solution(8487580849017899552)
XLA Ops:
  0.6 4.1 %collective-permute-start = (f32[1,32,8,128]{3,2,1,0:T(8,128)}, f32[1,32,8,128]{3,2,1,0:T(8,128)S(1)}, u32[]{:S(2)}, u32[]{:S(2)}) collective-permute-start(f32[1,32,8,128]{3,2,1,0:T(8,128)} %bitcast.59), channel_id=1, source_target_pairs={{0,16},{4,20},{8,24},{12,28},{16,0},{20,4},{24,8},{28,12},{1,17},{... | collective-permute-start | bytes 393224 | tf_op jit(solution)/shard_map/ppermute | solution.py:242
  4.8 7.3 %exchange_1.1 = (f32[4,32,8,128]{3,2,1,0:T(8,128)}, s32[4,8,128]{2,1,0:T(8,128)}) custom-call(f32[32,8,128]{2,1,0:T(8,128)} %prior_ref.3, s32[1,128]{1,0:T(1,128)} %bitcast.70, s32[1,128]{1,0:T(1,128)} %bitcast.71, s32[4,128]{1,0:T(4,128)} %bitcast.69), custom_call_target="tpu_custom_call" | custom-call | tf_op jit(solution)/shard_map/exchange_1/pallas_call | solution.py:83
  12.1 1.1 %fusion.7 = (f32[32,1,512]{2,1,0:T(1,128)S(1)}, f32[32,1,512]{2,1,0:T(1,128)S(1)}) fusion(f32[32,2,512]{2,1,0:T(2,128)} %param.20), kind=kLoop, calls=%fused_computation.22 | loop fusion | bytes 262144 | tf_op jit(solution)/shard_map/slice | solution.py:549
  13.2 0.0 collective-permute-done
  13.2 0.9 %pad_maximum_fusion.3 = f32[2,32,8,128]{3,2,1,0:T(8,128)S(1)} fusion(f32[1,32,8,128]{3,2,1,0:T(8,128)S(1)} %collective-permute-done, f32[1,32,8,128]{3,2,1,0:T(8,128)} %bitcast.60), kind=kLoop, calls=%fused_computation.10 | loop fusion | flops 65536 | bytes 524288 | tf_op jit(solution)/shard_map/concatenate | solution.py:243
  14.1 1.6 %collective-permute-start.1 = (f32[2,32,8,128]{3,2,1,0:T(8,128)S(1)}, f32[2,32,8,128]{3,2,1,0:T(8,128)S(1)}, u32[]{:S(2)}, u32[]{:S(2)}) collective-permute-start(f32[2,32,8,128]{3,2,1,0:T(8,128)S(1)} %pad_maximum_fusion.3), channel_id=1, source_target_pairs={{0,8},{4,12},{8,0},{12,4},{16,24},{20,28},{24,16},{28,20},{1,9},{5... | collective-permute-start | bytes 786440 | tf_op jit(solution)/shard_map/ppermute | solution.py:242
  15.8 0.7 multiply_bitcast_fusion.2
  16.5 0.7 copy.25
  17.2 20.6 %route.1.x_ref = f32[4,64,512]{2,1,0:T(8,128)} custom-call(s32[1]{0:T(128)} %bitcast.basin_ref, f32[4,32,8,128]{3,2,1,0:T(8,128)} %get-tuple-element.9.coef_ref, s32[4,8,128]{2,1,0:T(8,128)} %get-tuple-element.10.given_ref, f32[32,8,128]{2,1,0:T(8,128)} %prior_ref.3, f32[6,32,128]{2,1,0:T(8,128)} %constant.20.clone.cos_ref, f32[128,128]{1,0:T(8,128)} %bitcast.62, ...), custom_call_target="tpu_custom_call" | custom-call | flops 40000000 | bytes 60000000 | tf_op jit(solution)/shard_map/route/pallas_call | solution.py:511
  37.9 0.0 collective-permute-done.1
  37.9 19.4 %observed_2.1 = f32[8,32,1024]{2,1,0:T(8,128)} custom-call(f32[4,64,512]{2,1,0:T(8,128)} %route.1.x_ref), custom_call_target="tpu_custom_call" | custom-call | tf_op jit(solution)/shard_map/observed_2/pallas_call | solution.py:168
  57.3 0.0 copy-start
  57.3 0.4 collective-permute-start.2
  57.8 0.1 reduce_sum.31
  57.9 1.3 %reduce_sum.30 = f32[1024]{0:T(1024)S(1)} reduce(f32[8,32,1024]{2,1,0:T(8,128)} %observed_2.1, f32[]{:T(128)} %constant.6.clone.1), dimensions={0,1}, to_apply=%region_0.0 | reduce | flops 261120 | bytes 1052676 | tf_op jit(solution)/shard_map/reduce_sum | solution.py:551
  59.2 0.0 copy-done
  59.2 0.1 fusion.2
  59.4 0.1 pad_maximum_fusion
  59.5 0.1 subtract_divide_fusion
  59.7 0.0 slice-start
  59.7 1.9 %fusion.8.x_ref = f32[4,72,256]{2,1,0:T(8,128)} fusion(f32[4,72,1024]{2,1,0:T(8,128)S(1)} %bitcast.54, f32[256,1024,1]{1,0,2:T(8,128)S(1)} %bitcast.56), kind=kOutput, calls=%fused_computation.23 | convolution fusion | flops 905969664 | bytes 2523136 | tf_op jit(solution)/shard_map/dot_general | solution.py:556
  61.5 13.1 %sum_4.1 = f32[4,72,256]{2,1,0:T(8,128)} custom-call(f32[4,72,256]{2,1,0:T(8,128)} %fusion.8.x_ref), custom_call_target="tpu_custom_call" | custom-call | tf_op jit(solution)/shard_map/sum_4/pallas_call | solution.py:228
  74.7 0.0 slice-done
  74.7 0.8 reshape_squeeze.3
  75.5 12.7 %solve.1 = f32[256,32]{1,0:T(8,128)} custom-call(f32[288,256]{1,0:T(8,128)} %bitcast.61), custom_call_target="tpu_custom_call" | custom-call | flops 40000000 | bytes 60000000 | tf_op jit(solution)/shard_map/solve/pallas_call | solution.py:561
  88.1 0.0 collective-permute-done.2
  88.2 0.1 reduce_sum.32
  88.3 0.1 pad_maximum_fusion.1
  88.4 0.2 fusion.1
  88.6 0.0 copy-start.1
  88.6 0.0 copy-start.2
  88.6 0.3 copy.16
  89.0 0.5 copy-done.1
  89.5 0.1 copy-done.2
  89.6 1.1 %convolution_add_fusion = f32[32,8,128]{2,0,1:T(8,128)S(1)} fusion(f32[8,128,256]{2,1,0:T(8,128)S(1)} %bitcast.58, f32[256,32]{1,0:T(8,128)S(1)} %copy-done.2, f32[32,8,128]{2,1,0:T(8,128)S(1)} %copy-done.1), kind=kOutput, calls=%fused_computation.1 | convolution fusion | flops 100696064 | bytes 1343488 | tf_op jit(solution)/shard_map/dot_general | solution.py:575
  90.7 0.7 copy.19
  (7 shorter events, 0.1 us)
Async XLA Ops:
  0.6 12.6 %collective-permute-start = (f32[1,32,8,128]{3,2,1,0:T(8,128)}, f32[1,32,8,128]{3,2,1,0:T(8,128)S(1)}, u32[]{:S(2)}, u32[]{:S(2)}) collective-permute-start(f32[1,32,8,128]{3,2,1,0:T(8,128)} %bitcast.59), channel_id=1, source_target_pairs={{0,16},{4,20},{8,24},{12,28},{16,0},{20,4},{24,8},{28,12},{1,17},{... | collective-permute-start | bytes 393224 | tf_op jit(solution)/shard_map/ppermute | solution.py:242
  14.1 23.7 %collective-permute-start.1 = (f32[2,32,8,128]{3,2,1,0:T(8,128)S(1)}, f32[2,32,8,128]{3,2,1,0:T(8,128)S(1)}, u32[]{:S(2)}, u32[]{:S(2)}) collective-permute-start(f32[2,32,8,128]{3,2,1,0:T(8,128)S(1)} %pad_maximum_fusion.3), channel_id=1, source_target_pairs={{0,8},{4,12},{8,0},{12,4},{16,24},{20,28},{24,16},{28,20},{1,9},{5... | collective-permute-start | bytes 786440 | tf_op jit(solution)/shard_map/ppermute | solution.py:242
  57.3 1.9 %copy-start = (f32[8,32,1024]{2,1,0:T(8,128)S(1)}, f32[8,32,1024]{2,1,0:T(8,128)}, u32[]{:S(2)}) copy-start(f32[8,32,1024]{2,1,0:T(8,128)} %observed_2.1) | copy-start | bytes 3145732
  57.3 30.8 %collective-permute-start.2 = (f32[4,32,8,128]{3,2,1,0:T(8,128)S(1)}, f32[4,32,8,128]{3,2,1,0:T(8,128)S(1)}, u32[]{:S(2)}, u32[]{:S(2)}) collective-permute-start(f32[4,32,8,128]{3,2,1,0:T(8,128)S(1)} %pad_maximum_fusion.2), channel_id=1, source_target_pairs={{0,4},{4,0},{8,12},{12,8},{16,20},{20,16},{24,28},{28,24},{1,5},{5... | collective-permute-start | bytes 1572872 | tf_op jit(solution)/shard_map/ppermute | solution.py:242
  59.7 15.0 %slice-start = ((f32[8,32,1024]{2,1,0:T(8,128)}), f32[1,32,1024]{2,1,0:T(8,128)S(1)}, s32[]{:S(2)}) async-start(f32[8,32,1024]{2,1,0:T(8,128)} %observed_2.1), calls=%async_computation | async-start | bytes 262144 | tf_op jit(solution)/shard_map/slice | solution.py:543
  88.6 0.9 copy-start.1
  88.6 1.0 %copy-start.2 = (f32[256,32]{1,0:T(8,128)S(1)}, f32[256,32]{1,0:T(8,128)}, u32[]{:S(2)}) copy-start(f32[256,32]{1,0:T(8,128)} %solve.1) | copy-start | bytes 98308

commit v3 on v2

--- a/solution.py
+++ b/solution.py
@@ -107,42 +107,57 @@
     return bits
 
 
-def observed_body(
-    hours, n_basin, n, x_ref, o_ref, land_ref, part_send, part_recv, send_sem, recv_sem
+def assimilate_body(
+    hours, n_basin, n, padded,
+    x_ref, obs_ref, var_ref, noise_ref, pred_ref, sums_ref,
+    all_ref, land_ref, high_ref, low_ref, part_ref, land_g, land_c,
+    part_send, part_recv, send_sem, recv_sem,
+    gram_send, gram_recv, cross_send, cross_recv,
+    gram_out, gram_in, cross_out, cross_in, side_out, side_in,
 ):
     basin = lax.axis_index("basin")
     me = lax.axis_index("member")
+    rows = all_ref.shape[1]
+    gauges = x_ref.shape[2]
+    members = n * rows
     partners = [me + bit * (1 - 2 * lax.rem(me // bit, 2)) for bit in doubling_bits(n)]
     barrier = pltpu.get_barrier_semaphore()
     for i in range(1, n_basin):
-        pl.semaphore_signal(
-            barrier, inc=1, device_id={"basin": lax.rem(basin + i, n_basin)}, device_id_type=MESH
-        )
+        @pl.when(basin - i >= 0)
+        def _():
+            pl.semaphore_signal(
+                barrier, inc=1, device_id={"basin": lax.rem(basin - i + n_basin, n_basin)},
+                device_id_type=MESH,
+            )
     for partner in partners:
         pl.semaphore_signal(barrier, inc=1, device_id={"member": partner}, device_id_type=MESH)
-    pl.semaphore_wait(barrier, n_basin - 1 + len(partners))
-    parts = []
+    pl.semaphore_wait(barrier, n_basin - 1 - basin + len(partners))
+
+    def part_copy(i):
+        peer = lax.rem(basin + i, n_basin)
+        return pltpu.make_async_remote_copy(
+            src_ref=x_ref.at[peer], dst_ref=land_ref.at[i - 1],
+            send_sem=part_send.at[i - 1], recv_sem=part_recv.at[i - 1],
+            device_id={"basin": peer}, device_id_type=MESH,
+        )
+
+    for i in range(n_basin - 1, 0, -1):
+        @pl.when(basin + i < n_basin)
+        def _():
+            part_copy(i).start()
+
+    spread = 2.0 * jnp.sqrt(var_ref[...])
+    for h in range(hours):
+        span = slice(h * gauges, (h + 1) * gauges)
+        all_ref[0, :, span] = x_ref[basin, h * rows : (h + 1) * rows, :]
     for i in range(1, n_basin):
-        peer = lax.rem(basin + i, n_basin)
-        parts.append(
-            pltpu.make_async_remote_copy(
-                src_ref=x_ref.at[peer], dst_ref=land_ref.at[i - 1],
-                send_sem=part_send.at[i - 1], recv_sem=part_recv.at[i - 1],
-                device_id={"basin": peer}, device_id_type=MESH,
-            )
-        )
-    for copy in parts:
-        copy.start()
-    for copy in parts:
-        copy.wait()
-    flows = x_ref[basin]
-    for i in range(1, n_basin):
-        flows = flows + land_ref[i - 1]
-    pred = inverse_sinh(flows)
-    rows = o_ref.shape[1]
-    gauges = x_ref.shape[2]
-    for h in range(hours):
-        o_ref[0, :, h * gauges : (h + 1) * gauges] = pred[h * rows : (h + 1) * rows]
+        @pl.when(basin - i >= 0)
+        def _():
+            part_copy(i).wait_recv()
+            for h in range(hours):
+                span = slice(h * gauges, (h + 1) * gauges)
+                all_ref[0, :, span] += land_ref[i - 1, h * rows : (h + 1) * rows, :]
+    all_ref[0] = inverse_sinh(all_ref[0])
 
     copies = {}
     for p in range(n):
@@ -152,89 +167,177 @@
             to = 2**k + p
             if p < 2**k:
                 copies[to] = pltpu.make_async_remote_copy(
-                    src_ref=o_ref.at[p], dst_ref=o_ref.at[to],
+                    src_ref=all_ref.at[p], dst_ref=all_ref.at[to],
                     send_sem=send_sem.at[to - 1], recv_sem=recv_sem.at[to - 1],
                     device_id={"member": partner}, device_id_type=MESH,
                 )
                 copies[to].start()
+        if p == 0:
+            for h in range(hours):
+                span = slice(h * gauges, (h + 1) * gauges)
+                wide = spread[h : h + 1, :]
+                flow = all_ref[0, :, span]
+                pred_ref[:, h, :] = flow
+                away = (obs_ref[h : h + 1, :] + wide * noise_ref[:, h, :] - flow) / wide
+                high = away.astype(jnp.bfloat16)
+                high_ref[members : members + rows, span] = high
+                low_ref[members : members + rows, span] = (
+                    away - high.astype(jnp.float32)
+                ).astype(jnp.bfloat16)
     for p in range(1, n):
         copies[p].wait_send()
-
-
-def observed_gather(parts, hours, collective_id):
+    for i in range(1, n_basin):
+        @pl.when(basin + i < n_basin)
+        def _():
+            part_copy(i).wait_send()
+
+    for h in range(hours):
+        span = slice(h * gauges, (h + 1) * gauges)
+        total = all_ref[0, :, span]
+        for p in range(1, n):
+            total = total + all_ref[p, :, span]
+        mean = jnp.sum(total, 0, keepdims=True) / members
+        over = math.sqrt(members - 1.0) * spread[h : h + 1, :]
+        for p in range(n):
+            scaled = (all_ref[p, :, span] - mean) / over
+            high = scaled.astype(jnp.bfloat16)
+            high_ref[p * rows : (p + 1) * rows, span] = high
+            low_ref[p * rows : (p + 1) * rows, span] = (
+                scaled - high.astype(jnp.float32)
+            ).astype(jnp.bfloat16)
+
+    def product(a, b):
+        return lax.dot_general(
+            a, b, (((1,), (1,)), ((), ())), preferred_element_type=jnp.float32
+        )
+
+    used = members + rows
+    part_ref[:used, :] = (
+        product(high_ref[...], high_ref[:members, :])
+        + product(high_ref[...], low_ref[:members, :])
+        + product(low_ref[...], high_ref[:members, :])
+    )
+    if padded > rows:
+        part_ref[used:, :] = jnp.zeros((padded - rows, members), jnp.float32)
+
+    piece_g = members // (2 * n_basin)
+    piece_c = padded // n_basin
+
+    def gram_rows(side, which):
+        return pl.ds(pl.multiple_of((side * n_basin + which) * piece_g, piece_g), piece_g)
+
+    def cross_rows(which):
+        return pl.ds(pl.multiple_of(members + which * piece_c, piece_c), piece_c)
+
+    first = []
+    for i in range(1, n_basin):
+        peer = lax.rem(basin + i, n_basin)
+        for src, dst, out_sem, in_sem in (
+            (part_ref.at[gram_rows(0, peer)], land_g.at[i - 1], gram_send, gram_recv),
+            (part_ref.at[cross_rows(peer)], land_c.at[i - 1], cross_send, cross_recv),
+        ):
+            first.append(
+                pltpu.make_async_remote_copy(
+                    src_ref=src, dst_ref=dst,
+                    send_sem=out_sem.at[i - 1], recv_sem=in_sem.at[i - 1],
+                    device_id={"basin": peer}, device_id_type=MESH,
+                )
+            )
+    for copy in first:
+        copy.start()
+    for copy in first:
+        copy.wait_recv()
+    total_g = part_ref[gram_rows(0, basin), :]
+    total_c = part_ref[cross_rows(basin), :]
+    for i in range(1, n_basin):
+        total_g = total_g + land_g[i - 1]
+        total_c = total_c + land_c[i - 1]
+    sums_ref[gram_rows(0, basin), :] = total_g
+    sums_ref[cross_rows(basin), :] = total_c
+
+    def spread_copy(span, i, out_sem, in_sem):
+        return pltpu.make_async_remote_copy(
+            src_ref=sums_ref.at[span], dst_ref=sums_ref.at[span],
+            send_sem=out_sem.at[i - 1], recv_sem=in_sem.at[i - 1],
+            device_id={"basin": lax.rem(basin + i, n_basin)}, device_id_type=MESH,
+        )
+
+    half = members // 2
+
+    def side_copies(i):
+        which = lax.rem(basin - i + n_basin, n_basin)
+        return [
+            pltpu.make_async_remote_copy(
+                src_ref=sums_ref.at[gram_rows(0, which), a * half : (a + 1) * half],
+                dst_ref=sums_ref.at[gram_rows(1, which), (1 - a) * half : (2 - a) * half],
+                send_sem=side_out.at[i, a], recv_sem=side_in.at[i, a],
+                device_id={"member": partners[-1]}, device_id_type=MESH,
+            )
+            for a in range(2)
+        ]
+
+    second = []
+    for i in range(1, n_basin):
+        second.append(
+            (spread_copy(gram_rows(0, basin), i, gram_out, gram_in),
+             spread_copy(cross_rows(basin), i, cross_out, cross_in))
+        )
+    for pair in second:
+        for copy in pair:
+            copy.start()
+    sides = side_copies(0)
+    for copy in sides:
+        copy.start()
+    for i in range(1, n_basin):
+        second[i - 1][0].wait_recv()
+        passed = side_copies(i)
+        for copy in passed:
+            copy.start()
+        sides = sides + passed
+    for pair in second:
+        pair[1].wait_recv()
+    for copy in sides:
+        copy.wait_recv()
+    for copy in first + sides:
+        copy.wait_send()
+    for pair in second:
+        for copy in pair:
+            copy.wait_send()
+
+
+def assimilate(parts, observed, obs_var, obs_noise, collective_id):
     n = lax.axis_size("member")
-    n_basin = lax.axis_size("basin")
-    rows, gauges = parts.shape[1] // hours, parts.shape[2]
+    nb = lax.axis_size("basin")
+    rows, hours, gauges = obs_noise.shape
+    width = hours * gauges
+    members = n * rows
+    padded = rows + -rows % (8 * nb)
+    f32, bf16 = jnp.float32, jnp.bfloat16
+    dma = pltpu.SemaphoreType.DMA
     return pl.pallas_call(
-        functools.partial(observed_body, hours, n_basin, n),
-        out_shape=jax.ShapeDtypeStruct((n, rows, hours * gauges), parts.dtype),
-        in_specs=[vmem_spec()],
-        out_specs=vmem_spec(),
+        functools.partial(assimilate_body, hours, nb, n, padded),
+        out_shape=(
+            jax.ShapeDtypeStruct((rows, hours, gauges), f32),
+            jax.ShapeDtypeStruct((members + padded, members), f32),
+        ),
+        in_specs=[vmem_spec()] * 4,
+        out_specs=(vmem_spec(), vmem_spec()),
         scratch_shapes=[
-            VMEM((n_basin - 1,) + parts.shape[1:], parts.dtype),
-            pltpu.SemaphoreType.DMA((n_basin - 1,)),
-            pltpu.SemaphoreType.DMA((n_basin - 1,)),
-            pltpu.SemaphoreType.DMA((n - 1,)),
-            pltpu.SemaphoreType.DMA((n - 1,)),
-        ],
+            VMEM((n, rows, width), f32),
+            VMEM((nb - 1,) + parts.shape[1:], f32),
+            VMEM((members + rows, width), bf16),
+            VMEM((members + rows, width), bf16),
+            VMEM((members + padded, members), f32),
+            VMEM((nb - 1, members // (2 * nb), members), f32),
+            VMEM((nb - 1, padded // nb, members), f32),
+        ]
+        + [dma((nb - 1,))] * 2
+        + [dma((n - 1,))] * 2
+        + [dma((nb - 1,))] * 8
+        + [dma((nb, 2))] * 2,
         compiler_params=pltpu.CompilerParams(collective_id=collective_id, has_side_effects=True),
-        name=f"observed_{collective_id}",
-    )(parts)
-
-
-def sum_body(axis, n, x_ref, o_ref, land_ref, sem1, sem2, sem3, sem4):
-    me = lax.axis_index(axis)
-    barrier = pltpu.get_barrier_semaphore()
-    for i in range(1, n):
-        pl.semaphore_signal(
-            barrier, inc=1, device_id={axis: lax.rem(me + i, n)}, device_id_type=MESH
-        )
-    pl.semaphore_wait(barrier, n - 1)
-    copies = []
-    for i in range(1, n):
-        peer = lax.rem(me + i, n)
-        copies.append(
-            pltpu.make_async_remote_copy(
-                src_ref=x_ref.at[peer], dst_ref=land_ref.at[i - 1],
-                send_sem=sem1.at[i - 1], recv_sem=sem2.at[i - 1],
-                device_id={axis: peer}, device_id_type=MESH,
-            )
-        )
-    for copy in copies:
-        copy.start()
-    for copy in copies:
-        copy.wait()
-    total = x_ref[me]
-    for i in range(1, n):
-        total = total + land_ref[i - 1]
-    o_ref[me] = total
-    copies = []
-    for i in range(1, n):
-        copies.append(
-            pltpu.make_async_remote_copy(
-                src_ref=o_ref.at[me], dst_ref=o_ref.at[me],
-                send_sem=sem3.at[i - 1], recv_sem=sem4.at[i - 1],
-                device_id={axis: lax.rem(me + i, n)}, device_id_type=MESH,
-            )
-        )
-    for copy in copies:
-        copy.start()
-    for copy in copies:
-        copy.wait()
-
-
-def sum_over(x, axis, collective_id):
-    n = lax.axis_size(axis)
-    return pl.pallas_call(
-        functools.partial(sum_body, axis, n),
-        out_shape=jax.ShapeDtypeStruct(x.shape, x.dtype),
-        in_specs=[vmem_spec()],
-        out_specs=vmem_spec(),
-        scratch_shapes=[VMEM((n - 1,) + x.shape[1:], x.dtype)]
-        + [pltpu.SemaphoreType.DMA((n - 1,))] * 4,
-        compiler_params=pltpu.CompilerParams(collective_id=collective_id, has_side_effects=True),
-        name=f"sum_{collective_id}",
-    )(x)
+        name=f"assimilate_{collective_id}",
+    )(parts, observed, obs_var, obs_noise)
 
 
 def permuted_step(held, axis, bit):
@@ -539,25 +642,8 @@
     parts, held = lax.optimization_barrier((parts, held))
     held = permuted_step(held, "member", prior_steps[-1])
     prior_all = held.reshape(members, param_count * block_dev)
-    gathered = observed_gather(parts, hours, 2)
-    flat = gathered[0]
-    predicted = flat.reshape(md, hours, gauges)
-    pred_all = gathered.reshape(members, hours * gauges)
-
-    spread = jnp.sqrt(obs_var).reshape(1, -1)
+    predicted, sums = assimilate(parts, observed, obs_var, obs_noise, 2)
     spread_root = math.sqrt(members - 1.0)
-    noise = jnp.concatenate([obs_noise[:, h] for h in range(hours)], axis=1)
-    innovation = (observed.reshape(1, -1) + 2.0 * spread * noise - flat) / (2.0 * spread)
-    mean_pred = jnp.sum(pred_all, 0, keepdims=True) / members
-    scaled_all = (pred_all - mean_pred) / (spread_root * (2.0 * spread))
-    row_count = members + md
-    extra = -row_count % (8 * basins)
-    both = jnp.concatenate([scaled_all, innovation, jnp.zeros((extra, flat.shape[1]), f32)], 0)
-    part = lax.dot_general(
-        both, scaled_all, (((1,), (1,)), ((), ())),
-        precision=exact_mode, preferred_element_type=f32,
-    )
-    sums = sum_over(part.reshape(basins, -1, members), "basin", 4).reshape(-1, members)
     gain = pl.pallas_call(
         functools.partial(solve_body, n_member, md),
         out_shape=jax.ShapeDtypeStruct((members, md), f32),

time: 92.1 us -> 84 us (0.912)
  local copies, waits for them, and re-layouts: 4.26 us -> 1.81 us
  other arithmetic: 3.98 us -> 1.56 us
  matrix products: 2.96 us -> 1.11 us
  Pallas kernels: 73.2 us -> 72 us
    dot_general x1 -> x0, matrix products: 1.85 us -> none  [shards(): lax.dot_general(both, scaled_all, (((1,), (1,)), ((), ())), precision=exa...]
    reduce_sum x1 -> x0, other arithmetic: 1.3 us -> none  [shards(): mean_pred = jnp.sum(pred_all, 0, keepdims=True) / members]
    slice x3 -> x0, local copies, waits for them, and re-layouts: 1.1 us -> none  [the longest x1 1.1 us: shards(): noise = jnp.concatenate([obs_noise[:, h] for h in range(hours)], axis=1)]
    pallas_call x2 -> x1, Pallas kernels: 32.5 us -> 31.5 us  [assimilate(): pl.pallas_call(functools.partial(assimilate_body, hours, nb, n, padded),...]
    unnamed x10 -> x8, local copies, waits for them, and re-layouts: 2.05 us -> 1.48 us
  transfers between devices with their start and end apart: 3 -> 3, of which waited for: 0 -> 0; matrix products, arithmetic and copies ran while one was open for 8% -> 0% of each run, Pallas kernels for 59% -> 87%
where the time goes in v3:
time: 84 us; the launch traced here: 83.1 us
  Pallas kernels  72 us (86%)
  starting transfers between devices  5.84 us (7%)
  local copies, waits for them, and re-layouts  1.81 us (2%)
  other arithmetic  1.56 us (2%)
  matrix products  1.11 us (1%)
    pallas_call x1, Pallas kernels, assimilate(): pl.pallas_call(functools.partial(assimilate_body, hours, nb, n, padded),...  31.5 us
    pallas_call x1, Pallas kernels, shards(): pl.pallas_call(functools.partial(route_body, basins, level_count, md, gau...  20.5 us
    pallas_call x1, Pallas kernels, shards(): pl.pallas_call(functools.partial(solve_body, n_member, md), out_shape=jax...  12.7 us
    pallas_call x1, Pallas kernels, exchange(): pl.pallas_call(functools.partial(exchange_body, n), out_shape=(jax.ShapeD...  7.34 us
    ppermute x3, starting transfers between devices, permuted_step(): other = lax.ppermute(held, axis, [(i, i ^ bit) for i in range(n)])  5.84 us
  transfers between devices with their start and end apart: 3, of which 0 were waited for; matrix products, arithmetic and copies ran while one was open for 0% of the time, Pallas kernels for 87%

profile of v3, /device:TPU:0, one launch (start us, length us, event | category | flops | bytes accessed | tf_op | source)
XLA Modules:
  0.0 83.1 jit_solution(9101672640312275177)
XLA Ops:
  0.6 4.1 %collective-permute-start = (f32[1,32,8,128]{3,2,1,0:T(8,128)}, f32[1,32,8,128]{3,2,1,0:T(8,128)S(1)}, u32[]{:S(2)}, u32[]{:S(2)}) collective-permute-start(f32[1,32,8,128]{3,2,1,0:T(8,128)} %bitcast.32), channel_id=1, source_target_pairs={{0,16},{4,20},{8,24},{12,28},{16,0},{20,4},{24,8},{28,12},{1,17},{... | collective-permute-start | bytes 393224 | tf_op jit(solution)/shard_map/ppermute | solution.py:345
  4.8 7.3 %exchange_1.1 = (f32[4,32,8,128]{3,2,1,0:T(8,128)}, s32[4,8,128]{2,1,0:T(8,128)}) custom-call(f32[32,8,128]{2,1,0:T(8,128)} %prior_ref.3, s32[1,128]{1,0:T(1,128)} %bitcast.37, s32[1,128]{1,0:T(1,128)} %bitcast.38, s32[4,128]{1,0:T(4,128)} %bitcast.36), custom_call_target="tpu_custom_call" | custom-call | tf_op jit(solution)/shard_map/exchange_1/pallas_call | solution.py:83
  12.1 0.0 collective-permute-done
  12.1 0.9 %pad_maximum_fusion.2 = f32[2,32,8,128]{3,2,1,0:T(8,128)S(1)} fusion(f32[1,32,8,128]{3,2,1,0:T(8,128)S(1)} %collective-permute-done, f32[1,32,8,128]{3,2,1,0:T(8,128)} %bitcast.33), kind=kLoop, calls=%fused_computation.6 | loop fusion | flops 65536 | bytes 524288 | tf_op jit(solution)/shard_map/concatenate | solution.py:346
  13.0 1.6 %collective-permute-start.1 = (f32[2,32,8,128]{3,2,1,0:T(8,128)S(1)}, f32[2,32,8,128]{3,2,1,0:T(8,128)S(1)}, u32[]{:S(2)}, u32[]{:S(2)}) collective-permute-start(f32[2,32,8,128]{3,2,1,0:T(8,128)S(1)} %pad_maximum_fusion.2), channel_id=1, source_target_pairs={{0,8},{4,12},{8,0},{12,4},{16,24},{20,28},{24,16},{28,20},{1,9},{5... | collective-permute-start | bytes 786440 | tf_op jit(solution)/shard_map/ppermute | solution.py:345
  14.7 20.5 %route.1.x_ref = f32[4,64,512]{2,1,0:T(8,128)} custom-call(s32[1]{0:T(128)} %bitcast.basin_ref, f32[4,32,8,128]{3,2,1,0:T(8,128)} %get-tuple-element.11.coef_ref, s32[4,8,128]{2,1,0:T(8,128)} %get-tuple-element.12.given_ref, f32[32,8,128]{2,1,0:T(8,128)} %prior_ref.3, f32[6,32,128]{2,1,0:T(8,128)} %constant.14.clone.cos_ref, f32[128,128]{1,0:T(8,128)} %bitcast.34, ...), custom_call_target="tpu_custom_call" | custom-call | flops 40000000 | bytes 60000000 | tf_op jit(solution)/shard_map/route/pallas_call | solution.py:614
  35.2 0.0 collective-permute-done.1
  35.2 0.0 copy-start
  35.2 0.1 collective-permute-start.2
  35.3 0.1 reduce_sum.21
  35.4 31.5 %assimilate_2.1 = (f32[32,2,512]{2,1,0:T(2,128)}, f32[288,256]{1,0:T(8,128)}) custom-call(f32[4,64,512]{2,1,0:T(8,128)} %route.1.x_ref, f32[2,512]{1,0:T(2,128)} %obs_ref.1, f32[2,512]{1,0:T(2,128)} %var_ref.1, f32[32,2,512]{2,1,0:T(2,128)} %noise_ref.1), custom_call_target="tpu_custom_call" | custom-call | tf_op jit(solution)/shard_map/assimilate_2/pallas_call | solution.py:317
  67.0 12.7 %solve.1 = f32[256,32]{1,0:T(8,128)} custom-call(f32[288,256]{1,0:T(8,128)} %get-tuple-element.15.sums_ref), custom_call_target="tpu_custom_call" | custom-call | flops 40000000 | bytes 60000000 | tf_op jit(solution)/shard_map/solve/pallas_call | solution.py:647
  79.7 0.0 copy-start.1
  79.7 0.0 copy-start.2
  79.7 0.0 collective-permute-done.2
  79.7 0.1 reduce_sum.22
  79.8 0.1 pad_maximum_fusion
  79.9 0.2 fusion.1
  80.1 0.3 copy.14
  80.5 0.0 copy-done
  80.5 0.1 copy-done.1
  80.6 1.1 %convolution_add_fusion = f32[32,8,128]{2,0,1:T(8,128)S(1)} fusion(f32[8,128,256]{2,1,0:T(8,128)S(1)} %bitcast.31, f32[256,32]{1,0:T(8,128)S(1)} %copy-done.1, f32[32,8,128]{2,1,0:T(8,128)S(1)} %copy-done), kind=kOutput, calls=%fused_computation | convolution fusion | flops 100696064 | bytes 1343488 | tf_op jit(solution)/shard_map/dot_general | solution.py:661
  81.7 0.7 copy.17
  82.4 0.0 copy-done.2
  82.4 0.7 copy.24
  (2 shorter events, 0.0 us)
Async XLA Ops:
  0.6 11.5 %collective-permute-start = (f32[1,32,8,128]{3,2,1,0:T(8,128)}, f32[1,32,8,128]{3,2,1,0:T(8,128)S(1)}, u32[]{:S(2)}, u32[]{:S(2)}) collective-permute-start(f32[1,32,8,128]{3,2,1,0:T(8,128)} %bitcast.32), channel_id=1, source_target_pairs={{0,16},{4,20},{8,24},{12,28},{16,0},{20,4},{24,8},{28,12},{1,17},{... | collective-permute-start | bytes 393224 | tf_op jit(solution)/shard_map/ppermute | solution.py:345
  13.0 22.1 %collective-permute-start.1 = (f32[2,32,8,128]{3,2,1,0:T(8,128)S(1)}, f32[2,32,8,128]{3,2,1,0:T(8,128)S(1)}, u32[]{:S(2)}, u32[]{:S(2)}) collective-permute-start(f32[2,32,8,128]{3,2,1,0:T(8,128)S(1)} %pad_maximum_fusion.2), channel_id=1, source_target_pairs={{0,8},{4,12},{8,0},{12,4},{16,24},{20,28},{24,16},{28,20},{1,9},{5... | collective-permute-start | bytes 786440 | tf_op jit(solution)/shard_map/ppermute | solution.py:345
  35.2 45.3 %copy-start = (f32[32,8,128]{2,1,0:T(8,128)S(1)}, f32[32,8,128]{2,1,0:T(8,128)}, u32[]{:S(2)}) copy-start(f32[32,8,128]{2,1,0:T(8,128)} %prior_ref.3) | copy-start | bytes 393220
  35.2 44.5 %collective-permute-start.2 = (f32[4,32,8,128]{3,2,1,0:T(8,128)S(1)}, f32[4,32,8,128]{3,2,1,0:T(8,128)S(1)}, u32[]{:S(2)}, u32[]{:S(2)}) collective-permute-start(f32[4,32,8,128]{3,2,1,0:T(8,128)S(1)} %pad_maximum_fusion.1), channel_id=1, source_target_pairs={{0,4},{4,0},{8,12},{12,8},{16,20},{20,16},{24,28},{28,24},{1,5},{5... | collective-permute-start | bytes 1572872 | tf_op jit(solution)/shard_map/ppermute | solution.py:345
  79.7 0.9 %copy-start.1 = (f32[256,32]{1,0:T(8,128)S(1)}, f32[256,32]{1,0:T(8,128)}, u32[]{:S(2)}) copy-start(f32[256,32]{1,0:T(8,128)} %solve.1) | copy-start | bytes 98308
  79.7 2.8 %copy-start.2 = (f32[32,2,512]{2,1,0:T(2,128)S(1)}, f32[32,2,512]{2,1,0:T(2,128)}, u32[]{:S(2)}) copy-start(f32[32,2,512]{2,1,0:T(2,128)} %get-tuple-element.23) | copy-start | bytes 393220

commit v4 on v3

--- a/solution.py
+++ b/solution.py
@@ -117,7 +117,7 @@
 ):
     basin = lax.axis_index("basin")
     me = lax.axis_index("member")
-    rows = all_ref.shape[1]
+    rows = all_ref.shape[2]
     gauges = x_ref.shape[2]
     members = n * rows
     partners = [me + bit * (1 - 2 * lax.rem(me // bit, 2)) for bit in doubling_bits(n)]
@@ -133,73 +133,69 @@
         pl.semaphore_signal(barrier, inc=1, device_id={"member": partner}, device_id_type=MESH)
     pl.semaphore_wait(barrier, n_basin - 1 - basin + len(partners))
 
-    def part_copy(i):
+    def part_copy(i, h):
         peer = lax.rem(basin + i, n_basin)
+        span = slice(h * rows, (h + 1) * rows)
         return pltpu.make_async_remote_copy(
-            src_ref=x_ref.at[peer], dst_ref=land_ref.at[i - 1],
-            send_sem=part_send.at[i - 1], recv_sem=part_recv.at[i - 1],
+            src_ref=x_ref.at[peer, span], dst_ref=land_ref.at[i - 1, span],
+            send_sem=part_send.at[i - 1, h], recv_sem=part_recv.at[i - 1, h],
             device_id={"basin": peer}, device_id_type=MESH,
         )
 
-    for i in range(n_basin - 1, 0, -1):
-        @pl.when(basin + i < n_basin)
-        def _():
-            part_copy(i).start()
-
-    spread = 2.0 * jnp.sqrt(var_ref[...])
     for h in range(hours):
-        span = slice(h * gauges, (h + 1) * gauges)
-        all_ref[0, :, span] = x_ref[basin, h * rows : (h + 1) * rows, :]
-    for i in range(1, n_basin):
-        @pl.when(basin - i >= 0)
-        def _():
-            part_copy(i).wait_recv()
-            for h in range(hours):
-                span = slice(h * gauges, (h + 1) * gauges)
-                all_ref[0, :, span] += land_ref[i - 1, h * rows : (h + 1) * rows, :]
-    all_ref[0] = inverse_sinh(all_ref[0])
+        for i in range(n_basin - 1, 0, -1):
+            @pl.when(basin + i < n_basin)
+            def _():
+                part_copy(i, h).start()
 
     copies = {}
-    for p in range(n):
-        if p:
-            copies[p].wait_recv()
+
+    def pass_on(p, h):
         for k, partner in enumerate(partners):
             to = 2**k + p
             if p < 2**k:
-                copies[to] = pltpu.make_async_remote_copy(
-                    src_ref=all_ref.at[p], dst_ref=all_ref.at[to],
-                    send_sem=send_sem.at[to - 1], recv_sem=recv_sem.at[to - 1],
+                copies[to, h] = pltpu.make_async_remote_copy(
+                    src_ref=all_ref.at[h, p], dst_ref=all_ref.at[h, to],
+                    send_sem=send_sem.at[to - 1, h], recv_sem=recv_sem.at[to - 1, h],
                     device_id={"member": partner}, device_id_type=MESH,
                 )
-                copies[to].start()
-        if p == 0:
-            for h in range(hours):
-                span = slice(h * gauges, (h + 1) * gauges)
-                wide = spread[h : h + 1, :]
-                flow = all_ref[0, :, span]
-                pred_ref[:, h, :] = flow
-                away = (obs_ref[h : h + 1, :] + wide * noise_ref[:, h, :] - flow) / wide
-                high = away.astype(jnp.bfloat16)
-                high_ref[members : members + rows, span] = high
-                low_ref[members : members + rows, span] = (
-                    away - high.astype(jnp.float32)
-                ).astype(jnp.bfloat16)
-    for p in range(1, n):
-        copies[p].wait_send()
-    for i in range(1, n_basin):
-        @pl.when(basin + i < n_basin)
-        def _():
-            part_copy(i).wait_send()
-
+                copies[to, h].start()
+
+    spread = 2.0 * jnp.sqrt(var_ref[...])
+    for h in range(hours):
+        all_ref[h, 0] = x_ref[basin, h * rows : (h + 1) * rows, :]
+        for i in range(1, n_basin):
+            @pl.when(basin - i >= 0)
+            def _():
+                part_copy(i, h).wait_recv()
+                all_ref[h, 0] += land_ref[i - 1, h * rows : (h + 1) * rows, :]
+        all_ref[h, 0] = inverse_sinh(all_ref[h, 0])
+        pass_on(0, h)
     for h in range(hours):
         span = slice(h * gauges, (h + 1) * gauges)
-        total = all_ref[0, :, span]
+        wide = spread[h : h + 1, :]
+        flow = all_ref[h, 0]
+        pred_ref[:, h, :] = flow
+        away = (obs_ref[h : h + 1, :] + wide * noise_ref[:, h, :] - flow) / wide
+        high = away.astype(jnp.bfloat16)
+        high_ref[members : members + rows, span] = high
+        low_ref[members : members + rows, span] = (
+            away - high.astype(jnp.float32)
+        ).astype(jnp.bfloat16)
+    for p in range(1, n):
+        for h in range(hours):
+            copies[p, h].wait_recv()
+            pass_on(p, h)
+
+    for h in range(hours):
+        span = slice(h * gauges, (h + 1) * gauges)
+        total = all_ref[h, 0]
         for p in range(1, n):
-            total = total + all_ref[p, :, span]
+            total = total + all_ref[h, p]
         mean = jnp.sum(total, 0, keepdims=True) / members
         over = math.sqrt(members - 1.0) * spread[h : h + 1, :]
         for p in range(n):
-            scaled = (all_ref[p, :, span] - mean) / over
+            scaled = (all_ref[h, p] - mean) / over
             high = scaled.astype(jnp.bfloat16)
             high_ref[p * rows : (p + 1) * rows, span] = high
             low_ref[p * rows : (p + 1) * rows, span] = (
@@ -298,8 +294,13 @@
         pair[1].wait_recv()
     for copy in sides:
         copy.wait_recv()
-    for copy in first + sides:
+    for copy in list(copies.values()) + first + sides:
         copy.wait_send()
+    for h in range(hours):
+        for i in range(1, n_basin):
+            @pl.when(basin + i < n_basin)
+            def _():
+                part_copy(i, h).wait_send()
     for pair in second:
         for copy in pair:
             copy.wait_send()
@@ -323,7 +324,7 @@
         in_specs=[vmem_spec()] * 4,
         out_specs=(vmem_spec(), vmem_spec()),
         scratch_shapes=[
-            VMEM((n, rows, width), f32),
+            VMEM((hours, n, rows, gauges), f32),
             VMEM((nb - 1,) + parts.shape[1:], f32),
             VMEM((members + rows, width), bf16),
             VMEM((members + rows, width), bf16),
@@ -331,8 +332,8 @@
             VMEM((nb - 1, members // (2 * nb), members), f32),
             VMEM((nb - 1, padded // nb, members), f32),
         ]
-        + [dma((nb - 1,))] * 2
-        + [dma((n - 1,))] * 2
+        + [dma((nb - 1, hours))] * 2
+        + [dma((n - 1, hours))] * 2
         + [dma((nb - 1,))] * 8
         + [dma((nb, 2))] * 2,
         compiler_params=pltpu.CompilerParams(collective_id=collective_id, has_side_effects=True),

time: 84 us -> 80.4 us (0.957)
  Pallas kernels: 72 us -> 69.1 us
    pallas_call x1, Pallas kernels: 31.5 us -> 28.7 us  [assimilate(): pl.pallas_call(functools.partial(assimilate_body, hours, nb, n, padded),...]
  transfers between devices with their start and end apart: 3 -> 3, of which waited for: 0 -> 0; matrix products, arithmetic and copies ran while one was open for 0% -> 0% of each run, Pallas kernels for 87% -> 86%
where the time goes in v4:
time: 80.4 us; the launch traced here: 80.2 us
  Pallas kernels  69.1 us (86%)
  starting transfers between devices  5.84 us (7%)
  local copies, waits for them, and re-layouts  1.81 us (2%)
  other arithmetic  1.56 us (2%)
  matrix products  1.11 us (1%)
    pallas_call x1, Pallas kernels, assimilate(): pl.pallas_call(functools.partial(assimilate_body, hours, nb, n, padded),...  28.7 us
    pallas_call x1, Pallas kernels, shards(): pl.pallas_call(functools.partial(route_body, basins, level_count, md, gau...  20.5 us
    pallas_call x1, Pallas kernels, shards(): pl.pallas_call(functools.partial(solve_body, n_member, md), out_shape=jax...  12.7 us
    pallas_call x1, Pallas kernels, exchange(): pl.pallas_call(functools.partial(exchange_body, n), out_shape=(jax.ShapeD...  7.34 us
    ppermute x3, starting transfers between devices, permuted_step(): other = lax.ppermute(held, axis, [(i, i ^ bit) for i in range(n)])  5.84 us
  transfers between devices with their start and end apart: 3, of which 0 were waited for; matrix products, arithmetic and copies ran while one was open for 0% of the time, Pallas kernels for 86%

profile of v4, /device:TPU:0, one launch (start us, length us, event | category | flops | bytes accessed | tf_op | source)
XLA Modules:
  0.0 80.2 jit_solution(2086565256889245106)
XLA Ops:
  0.6 4.1 %collective-permute-start = (f32[1,32,8,128]{3,2,1,0:T(8,128)}, f32[1,32,8,128]{3,2,1,0:T(8,128)S(1)}, u32[]{:S(2)}, u32[]{:S(2)}) collective-permute-start(f32[1,32,8,128]{3,2,1,0:T(8,128)} %bitcast.32), channel_id=1, source_target_pairs={{0,16},{4,20},{8,24},{12,28},{16,0},{20,4},{24,8},{28,12},{1,17},{... | collective-permute-start | bytes 393224 | tf_op jit(solution)/shard_map/ppermute | solution.py:346
  4.8 7.3 %exchange_1.1 = (f32[4,32,8,128]{3,2,1,0:T(8,128)}, s32[4,8,128]{2,1,0:T(8,128)}) custom-call(f32[32,8,128]{2,1,0:T(8,128)} %prior_ref.3, s32[1,128]{1,0:T(1,128)} %bitcast.37, s32[1,128]{1,0:T(1,128)} %bitcast.38, s32[4,128]{1,0:T(4,128)} %bitcast.36), custom_call_target="tpu_custom_call" | custom-call | tf_op jit(solution)/shard_map/exchange_1/pallas_call | solution.py:83
  12.1 0.0 collective-permute-done
  12.1 0.9 %pad_maximum_fusion.2 = f32[2,32,8,128]{3,2,1,0:T(8,128)S(1)} fusion(f32[1,32,8,128]{3,2,1,0:T(8,128)S(1)} %collective-permute-done, f32[1,32,8,128]{3,2,1,0:T(8,128)} %bitcast.33), kind=kLoop, calls=%fused_computation.6 | loop fusion | flops 65536 | bytes 524288 | tf_op jit(solution)/shard_map/concatenate | solution.py:347
  13.0 1.6 %collective-permute-start.1 = (f32[2,32,8,128]{3,2,1,0:T(8,128)S(1)}, f32[2,32,8,128]{3,2,1,0:T(8,128)S(1)}, u32[]{:S(2)}, u32[]{:S(2)}) collective-permute-start(f32[2,32,8,128]{3,2,1,0:T(8,128)S(1)} %pad_maximum_fusion.2), channel_id=1, source_target_pairs={{0,8},{4,12},{8,0},{12,4},{16,24},{20,28},{24,16},{28,20},{1,9},{5... | collective-permute-start | bytes 786440 | tf_op jit(solution)/shard_map/ppermute | solution.py:346
  14.7 20.5 %route.1.x_ref = f32[4,64,512]{2,1,0:T(8,128)} custom-call(s32[1]{0:T(128)} %bitcast.basin_ref, f32[4,32,8,128]{3,2,1,0:T(8,128)} %get-tuple-element.11.coef_ref, s32[4,8,128]{2,1,0:T(8,128)} %get-tuple-element.12.given_ref, f32[32,8,128]{2,1,0:T(8,128)} %prior_ref.3, f32[6,32,128]{2,1,0:T(8,128)} %constant.14.clone.cos_ref, f32[128,128]{1,0:T(8,128)} %bitcast.34, ...), custom_call_target="tpu_custom_call" | custom-call | flops 40000000 | bytes 60000000 | tf_op jit(solution)/shard_map/route/pallas_call | solution.py:615
  35.1 0.0 collective-permute-done.1
  35.2 0.0 copy-start
  35.2 0.1 collective-permute-start.2
  35.3 0.1 reduce_sum.21
  35.4 28.7 %assimilate_2.1 = (f32[32,2,512]{2,1,0:T(2,128)}, f32[288,256]{1,0:T(8,128)}) custom-call(f32[4,64,512]{2,1,0:T(8,128)} %route.1.x_ref, f32[2,512]{1,0:T(2,128)} %obs_ref.1, f32[2,512]{1,0:T(2,128)} %var_ref.1, f32[32,2,512]{2,1,0:T(2,128)} %noise_ref.1), custom_call_target="tpu_custom_call" | custom-call | tf_op jit(solution)/shard_map/assimilate_2/pallas_call | solution.py:318
  64.1 12.7 %solve.1 = f32[256,32]{1,0:T(8,128)} custom-call(f32[288,256]{1,0:T(8,128)} %get-tuple-element.15.sums_ref), custom_call_target="tpu_custom_call" | custom-call | flops 40000000 | bytes 60000000 | tf_op jit(solution)/shard_map/solve/pallas_call | solution.py:648
  76.8 0.0 copy-start.1
  76.8 0.0 copy-start.2
  76.8 0.0 collective-permute-done.2
  76.8 0.1 reduce_sum.22
  76.9 0.1 pad_maximum_fusion
  77.0 0.2 fusion.1
  77.2 0.3 copy.14
  77.6 0.0 copy-done
  77.6 0.1 copy-done.1
  77.7 1.1 %convolution_add_fusion = f32[32,8,128]{2,0,1:T(8,128)S(1)} fusion(f32[8,128,256]{2,1,0:T(8,128)S(1)} %bitcast.31, f32[256,32]{1,0:T(8,128)S(1)} %copy-done.1, f32[32,8,128]{2,1,0:T(8,128)S(1)} %copy-done), kind=kOutput, calls=%fused_computation | convolution fusion | flops 100696064 | bytes 1343488 | tf_op jit(solution)/shard_map/dot_general | solution.py:662
  78.8 0.7 copy.17
  79.5 0.0 copy-done.2
  79.5 0.7 copy.24
  (2 shorter events, 0.0 us)
Async XLA Ops:
  0.6 11.5 %collective-permute-start = (f32[1,32,8,128]{3,2,1,0:T(8,128)}, f32[1,32,8,128]{3,2,1,0:T(8,128)S(1)}, u32[]{:S(2)}, u32[]{:S(2)}) collective-permute-start(f32[1,32,8,128]{3,2,1,0:T(8,128)} %bitcast.32), channel_id=1, source_target_pairs={{0,16},{4,20},{8,24},{12,28},{16,0},{20,4},{24,8},{28,12},{1,17},{... | collective-permute-start | bytes 393224 | tf_op jit(solution)/shard_map/ppermute | solution.py:346
  13.0 22.1 %collective-permute-start.1 = (f32[2,32,8,128]{3,2,1,0:T(8,128)S(1)}, f32[2,32,8,128]{3,2,1,0:T(8,128)S(1)}, u32[]{:S(2)}, u32[]{:S(2)}) collective-permute-start(f32[2,32,8,128]{3,2,1,0:T(8,128)S(1)} %pad_maximum_fusion.2), channel_id=1, source_target_pairs={{0,8},{4,12},{8,0},{12,4},{16,24},{20,28},{24,16},{28,20},{1,9},{5... | collective-permute-start | bytes 786440 | tf_op jit(solution)/shard_map/ppermute | solution.py:346
  35.2 42.4 %copy-start = (f32[32,8,128]{2,1,0:T(8,128)S(1)}, f32[32,8,128]{2,1,0:T(8,128)}, u32[]{:S(2)}) copy-start(f32[32,8,128]{2,1,0:T(8,128)} %prior_ref.3) | copy-start | bytes 393220
  35.2 41.6 %collective-permute-start.2 = (f32[4,32,8,128]{3,2,1,0:T(8,128)S(1)}, f32[4,32,8,128]{3,2,1,0:T(8,128)S(1)}, u32[]{:S(2)}, u32[]{:S(2)}) collective-permute-start(f32[4,32,8,128]{3,2,1,0:T(8,128)S(1)} %pad_maximum_fusion.1), channel_id=1, source_target_pairs={{0,4},{4,0},{8,12},{12,8},{16,20},{20,16},{24,28},{28,24},{1,5},{5... | collective-permute-start | bytes 1572872 | tf_op jit(solution)/shard_map/ppermute | solution.py:346
  76.8 0.9 %copy-start.1 = (f32[256,32]{1,0:T(8,128)S(1)}, f32[256,32]{1,0:T(8,128)}, u32[]{:S(2)}) copy-start(f32[256,32]{1,0:T(8,128)} %solve.1) | copy-start | bytes 98308
  76.8 2.8 %copy-start.2 = (f32[32,2,512]{2,1,0:T(2,128)S(1)}, f32[32,2,512]{2,1,0:T(2,128)}, u32[]{:S(2)}) copy-start(f32[32,2,512]{2,1,0:T(2,128)} %get-tuple-element.23) | copy-start | bytes 393220

commit v5 on v4

--- a/solution.py
+++ b/solution.py
@@ -118,7 +118,8 @@
     basin = lax.axis_index("basin")
     me = lax.axis_index("member")
     rows = all_ref.shape[2]
-    gauges = x_ref.shape[2]
+    chunks, width = all_ref.shape[0], all_ref.shape[3]
+    splits = chunks // hours
     members = n * rows
     partners = [me + bit * (1 - 2 * lax.rem(me // bit, 2)) for bit in doubling_bits(n)]
     barrier = pltpu.get_barrier_semaphore()
@@ -133,16 +134,19 @@
         pl.semaphore_signal(barrier, inc=1, device_id={"member": partner}, device_id_type=MESH)
     pl.semaphore_wait(barrier, n_basin - 1 - basin + len(partners))
 
+    def place(h):
+        hour, split = h // splits, h % splits
+        return slice(hour * rows, (hour + 1) * rows), slice(split * width, (split + 1) * width)
+
     def part_copy(i, h):
         peer = lax.rem(basin + i, n_basin)
-        span = slice(h * rows, (h + 1) * rows)
         return pltpu.make_async_remote_copy(
-            src_ref=x_ref.at[peer, span], dst_ref=land_ref.at[i - 1, span],
+            src_ref=x_ref.at[(peer,) + place(h)], dst_ref=land_ref.at[i - 1, h],
             send_sem=part_send.at[i - 1, h], recv_sem=part_recv.at[i - 1, h],
             device_id={"basin": peer}, device_id_type=MESH,
         )
 
-    for h in range(hours):
+    for h in range(chunks):
         for i in range(n_basin - 1, 0, -1):
             @pl.when(basin + i < n_basin)
             def _():
@@ -162,38 +166,40 @@
                 copies[to, h].start()
 
     spread = 2.0 * jnp.sqrt(var_ref[...])
-    for h in range(hours):
-        all_ref[h, 0] = x_ref[basin, h * rows : (h + 1) * rows, :]
+    for h in range(chunks):
+        all_ref[h, 0] = x_ref[(basin,) + place(h)]
         for i in range(1, n_basin):
             @pl.when(basin - i >= 0)
             def _():
                 part_copy(i, h).wait_recv()
-                all_ref[h, 0] += land_ref[i - 1, h * rows : (h + 1) * rows, :]
+                all_ref[h, 0] += land_ref[i - 1, h]
         all_ref[h, 0] = inverse_sinh(all_ref[h, 0])
         pass_on(0, h)
-    for h in range(hours):
-        span = slice(h * gauges, (h + 1) * gauges)
-        wide = spread[h : h + 1, :]
+    for h in range(chunks):
+        span = slice(h * width, (h + 1) * width)
+        hour, cols = h // splits, place(h)[1]
+        wide = spread[hour : hour + 1, cols]
         flow = all_ref[h, 0]
-        pred_ref[:, h, :] = flow
-        away = (obs_ref[h : h + 1, :] + wide * noise_ref[:, h, :] - flow) / wide
+        pred_ref[:, hour, cols] = flow
+        away = (obs_ref[hour : hour + 1, cols] + wide * noise_ref[:, hour, cols] - flow) / wide
         high = away.astype(jnp.bfloat16)
         high_ref[members : members + rows, span] = high
         low_ref[members : members + rows, span] = (
             away - high.astype(jnp.float32)
         ).astype(jnp.bfloat16)
     for p in range(1, n):
-        for h in range(hours):
+        for h in range(chunks):
             copies[p, h].wait_recv()
             pass_on(p, h)
 
-    for h in range(hours):
-        span = slice(h * gauges, (h + 1) * gauges)
+    for h in range(chunks):
+        span = slice(h * width, (h + 1) * width)
+        hour, cols = h // splits, place(h)[1]
         total = all_ref[h, 0]
         for p in range(1, n):
             total = total + all_ref[h, p]
         mean = jnp.sum(total, 0, keepdims=True) / members
-        over = math.sqrt(members - 1.0) * spread[h : h + 1, :]
+        over = math.sqrt(members - 1.0) * spread[hour : hour + 1, cols]
         for p in range(n):
             scaled = (all_ref[h, p] - mean) / over
             high = scaled.astype(jnp.bfloat16)
@@ -296,7 +302,7 @@
         copy.wait_recv()
     for copy in list(copies.values()) + first + sides:
         copy.wait_send()
-    for h in range(hours):
+    for h in range(chunks):
         for i in range(1, n_basin):
             @pl.when(basin + i < n_basin)
             def _():
@@ -311,6 +317,7 @@
     nb = lax.axis_size("basin")
     rows, hours, gauges = obs_noise.shape
     width = hours * gauges
+    chunks = 2 * hours if gauges % (2 * LANES) == 0 else hours
     members = n * rows
     padded = rows + -rows % (8 * nb)
     f32, bf16 = jnp.float32, jnp.bfloat16
@@ -324,16 +331,16 @@
         in_specs=[vmem_spec()] * 4,
         out_specs=(vmem_spec(), vmem_spec()),
         scratch_shapes=[
-            VMEM((hours, n, rows, gauges), f32),
-            VMEM((nb - 1,) + parts.shape[1:], f32),
+            VMEM((chunks, n, rows, width // chunks), f32),
+            VMEM((nb - 1, chunks, rows, width // chunks), f32),
             VMEM((members + rows, width), bf16),
             VMEM((members + rows, width), bf16),
             VMEM((members + padded, members), f32),
             VMEM((nb - 1, members // (2 * nb), members), f32),
             VMEM((nb - 1, padded // nb, members), f32),
         ]
-        + [dma((nb - 1, hours))] * 2
-        + [dma((n - 1, hours))] * 2
+        + [dma((nb - 1, chunks))] * 2
+        + [dma((n - 1, chunks))] * 2
         + [dma((nb - 1,))] * 8
         + [dma((nb, 2))] * 2,
         compiler_params=pltpu.CompilerParams(collective_id=collective_id, has_side_effects=True),

time: 80.4 us -> 80.4 us (level)
  no operation moved by 1% of the time
where the time goes in v5:
time: 80.4 us; the launch traced here: 80.2 us
  Pallas kernels  69.1 us (86%)
  starting transfers between devices  5.84 us (7%)
  local copies, waits for them, and re-layouts  1.81 us (2%)
  other arithmetic  1.56 us (2%)
  matrix products  1.11 us (1%)
    pallas_call x1, Pallas kernels, assimilate(): pl.pallas_call(functools.partial(assimilate_body, hours, nb, n, padded),...  28.6 us
    pallas_call x1, Pallas kernels, shards(): pl.pallas_call(functools.partial(route_body, basins, level_count, md, gau...  20.4 us
    pallas_call x1, Pallas kernels, shards(): pl.pallas_call(functools.partial(solve_body, n_member, md), out_shape=jax...  12.7 us
    pallas_call x1, Pallas kernels, exchange(): pl.pallas_call(functools.partial(exchange_body, n), out_shape=(jax.ShapeD...  7.34 us
    ppermute x3, starting transfers between devices, permuted_step(): other = lax.ppermute(held, axis, [(i, i ^ bit) for i in range(n)])  5.84 us
  transfers between devices with their start and end apart: 3, of which 0 were waited for; matrix products, arithmetic and copies ran while one was open for 0% of the time, Pallas kernels for 86%

profile of v5, /device:TPU:0, one launch (start us, length us, event | category | flops | bytes accessed | tf_op | source)
XLA Modules:
  0.0 80.2 jit_solution(4784643150967382735)
XLA Ops:
  0.6 4.1 %collective-permute-start = (f32[1,32,8,128]{3,2,1,0:T(8,128)}, f32[1,32,8,128]{3,2,1,0:T(8,128)S(1)}, u32[]{:S(2)}, u32[]{:S(2)}) collective-permute-start(f32[1,32,8,128]{3,2,1,0:T(8,128)} %bitcast.32), channel_id=1, source_target_pairs={{0,16},{4,20},{8,24},{12,28},{16,0},{20,4},{24,8},{28,12},{1,17},{... | collective-permute-start | bytes 393224 | tf_op jit(solution)/shard_map/ppermute | solution.py:353
  4.8 7.3 %exchange_1.1 = (f32[4,32,8,128]{3,2,1,0:T(8,128)}, s32[4,8,128]{2,1,0:T(8,128)}) custom-call(f32[32,8,128]{2,1,0:T(8,128)} %prior_ref.3, s32[1,128]{1,0:T(1,128)} %bitcast.37, s32[1,128]{1,0:T(1,128)} %bitcast.38, s32[4,128]{1,0:T(4,128)} %bitcast.36), custom_call_target="tpu_custom_call" | custom-call | tf_op jit(solution)/shard_map/exchange_1/pallas_call | solution.py:83
  12.1 0.0 collective-permute-done
  12.1 0.9 %pad_maximum_fusion.2 = f32[2,32,8,128]{3,2,1,0:T(8,128)S(1)} fusion(f32[1,32,8,128]{3,2,1,0:T(8,128)S(1)} %collective-permute-done, f32[1,32,8,128]{3,2,1,0:T(8,128)} %bitcast.33), kind=kLoop, calls=%fused_computation.6 | loop fusion | flops 65536 | bytes 524288 | tf_op jit(solution)/shard_map/concatenate | solution.py:354
  13.0 1.6 %collective-permute-start.1 = (f32[2,32,8,128]{3,2,1,0:T(8,128)S(1)}, f32[2,32,8,128]{3,2,1,0:T(8,128)S(1)}, u32[]{:S(2)}, u32[]{:S(2)}) collective-permute-start(f32[2,32,8,128]{3,2,1,0:T(8,128)S(1)} %pad_maximum_fusion.2), channel_id=1, source_target_pairs={{0,8},{4,12},{8,0},{12,4},{16,24},{20,28},{24,16},{28,20},{1,9},{5... | collective-permute-start | bytes 786440 | tf_op jit(solution)/shard_map/ppermute | solution.py:353
  14.7 20.4 %route.1.x_ref = f32[4,64,512]{2,1,0:T(8,128)} custom-call(s32[1]{0:T(128)} %bitcast.basin_ref, f32[4,32,8,128]{3,2,1,0:T(8,128)} %get-tuple-element.11.coef_ref, s32[4,8,128]{2,1,0:T(8,128)} %get-tuple-element.12.given_ref, f32[32,8,128]{2,1,0:T(8,128)} %prior_ref.3, f32[6,32,128]{2,1,0:T(8,128)} %constant.14.clone.cos_ref, f32[128,128]{1,0:T(8,128)} %bitcast.34, ...), custom_call_target="tpu_custom_call" | custom-call | flops 40000000 | bytes 60000000 | tf_op jit(solution)/shard_map/route/pallas_call | solution.py:622
  35.1 0.0 collective-permute-done.1
  35.2 0.0 copy-start
  35.2 0.1 collective-permute-start.2
  35.3 0.1 reduce_sum.21
  35.4 28.6 %assimilate_2.1 = (f32[32,2,512]{2,1,0:T(2,128)}, f32[288,256]{1,0:T(8,128)}) custom-call(f32[4,64,512]{2,1,0:T(8,128)} %route.1.x_ref, f32[2,512]{1,0:T(2,128)} %obs_ref.1, f32[2,512]{1,0:T(2,128)} %var_ref.1, f32[32,2,512]{2,1,0:T(2,128)} %noise_ref.1), custom_call_target="tpu_custom_call" | custom-call | tf_op jit(solution)/shard_map/assimilate_2/pallas_call | solution.py:325
  64.1 12.7 %solve.1 = f32[256,32]{1,0:T(8,128)} custom-call(f32[288,256]{1,0:T(8,128)} %get-tuple-element.15.sums_ref), custom_call_target="tpu_custom_call" | custom-call | flops 40000000 | bytes 60000000 | tf_op jit(solution)/shard_map/solve/pallas_call | solution.py:655
  76.7 0.0 copy-start.1
  76.7 0.0 copy-start.2
  76.7 0.0 collective-permute-done.2
  76.7 0.1 reduce_sum.22
  76.9 0.1 pad_maximum_fusion
  77.0 0.2 fusion.1
  77.2 0.3 copy.14
  77.6 0.0 copy-done
  77.6 0.1 copy-done.1
  77.6 1.1 %convolution_add_fusion = f32[32,8,128]{2,0,1:T(8,128)S(1)} fusion(f32[8,128,256]{2,1,0:T(8,128)S(1)} %bitcast.31, f32[256,32]{1,0:T(8,128)S(1)} %copy-done.1, f32[32,8,128]{2,1,0:T(8,128)S(1)} %copy-done), kind=kOutput, calls=%fused_computation | convolution fusion | flops 100696064 | bytes 1343488 | tf_op jit(solution)/shard_map/dot_general | solution.py:669
  78.8 0.7 copy.17
  79.5 0.0 copy-done.2
  79.5 0.7 copy.24
  (2 shorter events, 0.0 us)
Async XLA Ops:
  0.6 11.5 %collective-permute-start = (f32[1,32,8,128]{3,2,1,0:T(8,128)}, f32[1,32,8,128]{3,2,1,0:T(8,128)S(1)}, u32[]{:S(2)}, u32[]{:S(2)}) collective-permute-start(f32[1,32,8,128]{3,2,1,0:T(8,128)} %bitcast.32), channel_id=1, source_target_pairs={{0,16},{4,20},{8,24},{12,28},{16,0},{20,4},{24,8},{28,12},{1,17},{... | collective-permute-start | bytes 393224 | tf_op jit(solution)/shard_map/ppermute | solution.py:353
  13.0 22.1 %collective-permute-start.1 = (f32[2,32,8,128]{3,2,1,0:T(8,128)S(1)}, f32[2,32,8,128]{3,2,1,0:T(8,128)S(1)}, u32[]{:S(2)}, u32[]{:S(2)}) collective-permute-start(f32[2,32,8,128]{3,2,1,0:T(8,128)S(1)} %pad_maximum_fusion.2), channel_id=1, source_target_pairs={{0,8},{4,12},{8,0},{12,4},{16,24},{20,28},{24,16},{28,20},{1,9},{5... | collective-permute-start | bytes 786440 | tf_op jit(solution)/shard_map/ppermute | solution.py:353
  35.2 42.4 %copy-start = (f32[32,8,128]{2,1,0:T(8,128)S(1)}, f32[32,8,128]{2,1,0:T(8,128)}, u32[]{:S(2)}) copy-start(f32[32,8,128]{2,1,0:T(8,128)} %prior_ref.3) | copy-start | bytes 393220
  35.2 41.5 %collective-permute-start.2 = (f32[4,32,8,128]{3,2,1,0:T(8,128)S(1)}, f32[4,32,8,128]{3,2,1,0:T(8,128)S(1)}, u32[]{:S(2)}, u32[]{:S(2)}) collective-permute-start(f32[4,32,8,128]{3,2,1,0:T(8,128)S(1)} %pad_maximum_fusion.1), channel_id=1, source_target_pairs={{0,4},{4,0},{8,12},{12,8},{16,20},{20,16},{24,28},{28,24},{1,5},{5... | collective-permute-start | bytes 1572872 | tf_op jit(solution)/shard_map/ppermute | solution.py:353
  76.7 0.9 %copy-start.1 = (f32[256,32]{1,0:T(8,128)S(1)}, f32[256,32]{1,0:T(8,128)}, u32[]{:S(2)}) copy-start(f32[256,32]{1,0:T(8,128)} %solve.1) | copy-start | bytes 98308
  76.7 2.8 %copy-start.2 = (f32[32,2,512]{2,1,0:T(2,128)S(1)}, f32[32,2,512]{2,1,0:T(2,128)}, u32[]{:S(2)}) copy-start(f32[32,2,512]{2,1,0:T(2,128)} %get-tuple-element.23) | copy-start | bytes 393220

commit v6 on v5

--- a/solution.py
+++ b/solution.py
@@ -636,7 +636,7 @@
             VMEM((block_dev, hours + 2, md, LANES), f32),
             VMEM(table_all.shape, jnp.int32),
             SMEM(table_all.shape, jnp.int32),
-            pltpu.SemaphoreType.DMA((4, md)),
+            pltpu.SemaphoreType.DMA((8, md)),
             pltpu.SemaphoreType.DMA,
         ],
         cost_estimate=pl.CostEstimate(

time: 80.4 us -> 82.1 us (1.021)
  Pallas kernels: 69.1 us -> 70.8 us
    pallas_call x1, Pallas kernels: 20.4 us -> 22.1 us  [shards(): pl.pallas_call(functools.partial(route_body, basins, level_count, md, gau...]
where the time goes in v6:
time: 82.1 us; the launch traced here: 81.9 us
  Pallas kernels  70.8 us (86%)
  starting transfers between devices  5.84 us (7%)
  local copies, waits for them, and re-layouts  1.81 us (2%)
  other arithmetic  1.56 us (2%)
  matrix products  1.11 us (1%)
    pallas_call x1, Pallas kernels, assimilate(): pl.pallas_call(functools.partial(assimilate_body, hours, nb, n, padded),...  28.6 us
    pallas_call x1, Pallas kernels, shards(): pl.pallas_call(functools.partial(route_body, basins, level_count, md, gau...  22.1 us
    pallas_call x1, Pallas kernels, shards(): pl.pallas_call(functools.partial(solve_body, n_member, md), out_shape=jax...  12.7 us
    pallas_call x1, Pallas kernels, exchange(): pl.pallas_call(functools.partial(exchange_body, n), out_shape=(jax.ShapeD...  7.34 us
    ppermute x3, starting transfers between devices, permuted_step(): other = lax.ppermute(held, axis, [(i, i ^ bit) for i in range(n)])  5.84 us
  transfers between devices with their start and end apart: 3, of which 0 were waited for; matrix products, arithmetic and copies ran while one was open for 0% of the time, Pallas kernels for 86%

profile of v6, /device:TPU:0, one launch (start us, length us, event | category | flops | bytes accessed | tf_op | source)
XLA Modules:
  0.0 81.9 jit_solution(10740373967007948342)
XLA Ops:
  0.6 4.1 %collective-permute-start = (f32[1,32,8,128]{3,2,1,0:T(8,128)}, f32[1,32,8,128]{3,2,1,0:T(8,128)S(1)}, u32[]{:S(2)}, u32[]{:S(2)}) collective-permute-start(f32[1,32,8,128]{3,2,1,0:T(8,128)} %bitcast.32), channel_id=1, source_target_pairs={{0,16},{4,20},{8,24},{12,28},{16,0},{20,4},{24,8},{28,12},{1,17},{... | collective-permute-start | bytes 393224 | tf_op jit(solution)/shard_map/ppermute | solution.py:353
  4.8 7.3 %exchange_1.1 = (f32[4,32,8,128]{3,2,1,0:T(8,128)}, s32[4,8,128]{2,1,0:T(8,128)}) custom-call(f32[32,8,128]{2,1,0:T(8,128)} %prior_ref.3, s32[1,128]{1,0:T(1,128)} %bitcast.37, s32[1,128]{1,0:T(1,128)} %bitcast.38, s32[4,128]{1,0:T(4,128)} %bitcast.36), custom_call_target="tpu_custom_call" | custom-call | tf_op jit(solution)/shard_map/exchange_1/pallas_call | solution.py:83
  12.1 0.0 collective-permute-done
  12.1 0.9 %pad_maximum_fusion.2 = f32[2,32,8,128]{3,2,1,0:T(8,128)S(1)} fusion(f32[1,32,8,128]{3,2,1,0:T(8,128)S(1)} %collective-permute-done, f32[1,32,8,128]{3,2,1,0:T(8,128)} %bitcast.33), kind=kLoop, calls=%fused_computation.6 | loop fusion | flops 65536 | bytes 524288 | tf_op jit(solution)/shard_map/concatenate | solution.py:354
  13.0 1.6 %collective-permute-start.1 = (f32[2,32,8,128]{3,2,1,0:T(8,128)S(1)}, f32[2,32,8,128]{3,2,1,0:T(8,128)S(1)}, u32[]{:S(2)}, u32[]{:S(2)}) collective-permute-start(f32[2,32,8,128]{3,2,1,0:T(8,128)S(1)} %pad_maximum_fusion.2), channel_id=1, source_target_pairs={{0,8},{4,12},{8,0},{12,4},{16,24},{20,28},{24,16},{28,20},{1,9},{5... | collective-permute-start | bytes 786440 | tf_op jit(solution)/shard_map/ppermute | solution.py:353
  14.7 22.1 %route.1.x_ref = f32[4,64,512]{2,1,0:T(8,128)} custom-call(s32[1]{0:T(128)} %bitcast.basin_ref, f32[4,32,8,128]{3,2,1,0:T(8,128)} %get-tuple-element.11.coef_ref, s32[4,8,128]{2,1,0:T(8,128)} %get-tuple-element.12.given_ref, f32[32,8,128]{2,1,0:T(8,128)} %prior_ref.3, f32[6,32,128]{2,1,0:T(8,128)} %constant.14.clone.cos_ref, f32[128,128]{1,0:T(8,128)} %bitcast.34, ...), custom_call_target="tpu_custom_call" | custom-call | flops 40000000 | bytes 60000000 | tf_op jit(solution)/shard_map/route/pallas_call | solution.py:622
  36.8 0.0 collective-permute-done.1
  36.9 0.0 copy-start
  36.9 0.1 collective-permute-start.2
  37.0 0.1 reduce_sum.21
  37.1 28.6 %assimilate_2.1 = (f32[32,2,512]{2,1,0:T(2,128)}, f32[288,256]{1,0:T(8,128)}) custom-call(f32[4,64,512]{2,1,0:T(8,128)} %route.1.x_ref, f32[2,512]{1,0:T(2,128)} %obs_ref.1, f32[2,512]{1,0:T(2,128)} %var_ref.1, f32[32,2,512]{2,1,0:T(2,128)} %noise_ref.1), custom_call_target="tpu_custom_call" | custom-call | tf_op jit(solution)/shard_map/assimilate_2/pallas_call | solution.py:325
  65.8 12.7 %solve.1 = f32[256,32]{1,0:T(8,128)} custom-call(f32[288,256]{1,0:T(8,128)} %get-tuple-element.15.sums_ref), custom_call_target="tpu_custom_call" | custom-call | flops 40000000 | bytes 60000000 | tf_op jit(solution)/shard_map/solve/pallas_call | solution.py:655
  78.4 0.0 copy-start.1
  78.4 0.0 copy-start.2
  78.4 0.0 collective-permute-done.2
  78.4 0.1 reduce_sum.22
  78.6 0.1 pad_maximum_fusion
  78.7 0.2 fusion.1
  78.9 0.3 copy.14
  79.3 0.0 copy-done
  79.3 0.1 copy-done.1
  79.3 1.1 %convolution_add_fusion = f32[32,8,128]{2,0,1:T(8,128)S(1)} fusion(f32[8,128,256]{2,1,0:T(8,128)S(1)} %bitcast.31, f32[256,32]{1,0:T(8,128)S(1)} %copy-done.1, f32[32,8,128]{2,1,0:T(8,128)S(1)} %copy-done), kind=kOutput, calls=%fused_computation | convolution fusion | flops 100696064 | bytes 1343488 | tf_op jit(solution)/shard_map/dot_general | solution.py:669
  80.5 0.7 copy.17
  81.2 0.0 copy-done.2
  81.2 0.7 copy.24
  (2 shorter events, 0.0 us)
Async XLA Ops:
  0.6 11.5 %collective-permute-start = (f32[1,32,8,128]{3,2,1,0:T(8,128)}, f32[1,32,8,128]{3,2,1,0:T(8,128)S(1)}, u32[]{:S(2)}, u32[]{:S(2)}) collective-permute-start(f32[1,32,8,128]{3,2,1,0:T(8,128)} %bitcast.32), channel_id=1, source_target_pairs={{0,16},{4,20},{8,24},{12,28},{16,0},{20,4},{24,8},{28,12},{1,17},{... | collective-permute-start | bytes 393224 | tf_op jit(solution)/shard_map/ppermute | solution.py:353
  13.0 23.8 %collective-permute-start.1 = (f32[2,32,8,128]{3,2,1,0:T(8,128)S(1)}, f32[2,32,8,128]{3,2,1,0:T(8,128)S(1)}, u32[]{:S(2)}, u32[]{:S(2)}) collective-permute-start(f32[2,32,8,128]{3,2,1,0:T(8,128)S(1)} %pad_maximum_fusion.2), channel_id=1, source_target_pairs={{0,8},{4,12},{8,0},{12,4},{16,24},{20,28},{24,16},{28,20},{1,9},{5... | collective-permute-start | bytes 786440 | tf_op jit(solution)/shard_map/ppermute | solution.py:353
  36.9 42.4 %copy-start = (f32[32,8,128]{2,1,0:T(8,128)S(1)}, f32[32,8,128]{2,1,0:T(8,128)}, u32[]{:S(2)}) copy-start(f32[32,8,128]{2,1,0:T(8,128)} %prior_ref.3) | copy-start | bytes 393220
  36.9 41.5 %collective-permute-start.2 = (f32[4,32,8,128]{3,2,1,0:T(8,128)S(1)}, f32[4,32,8,128]{3,2,1,0:T(8,128)S(1)}, u32[]{:S(2)}, u32[]{:S(2)}) collective-permute-start(f32[4,32,8,128]{3,2,1,0:T(8,128)S(1)} %pad_maximum_fusion.1), channel_id=1, source_target_pairs={{0,4},{4,0},{8,12},{12,8},{16,20},{20,16},{24,28},{28,24},{1,5},{5... | collective-permute-start | bytes 1572872 | tf_op jit(solution)/shard_map/ppermute | solution.py:353
  78.4 0.9 %copy-start.1 = (f32[256,32]{1,0:T(8,128)S(1)}, f32[256,32]{1,0:T(8,128)}, u32[]{:S(2)}) copy-start(f32[256,32]{1,0:T(8,128)} %solve.1) | copy-start | bytes 98308
  78.4 2.8 %copy-start.2 = (f32[32,2,512]{2,1,0:T(2,128)S(1)}, f32[32,2,512]{2,1,0:T(2,128)}, u32[]{:S(2)}) copy-start(f32[32,2,512]{2,1,0:T(2,128)} %get-tuple-element.23) | copy-start | bytes 393220

commit v7 on v6

--- a/solution.py
+++ b/solution.py
@@ -636,7 +636,7 @@
             VMEM((block_dev, hours + 2, md, LANES), f32),
             VMEM(table_all.shape, jnp.int32),
             SMEM(table_all.shape, jnp.int32),
-            pltpu.SemaphoreType.DMA((8, md)),
+            pltpu.SemaphoreType.DMA((2, md)),
             pltpu.SemaphoreType.DMA,
         ],
         cost_estimate=pl.CostEstimate(

time: 82.1 us -> 80 us (0.974)
  Pallas kernels: 70.8 us -> 68.7 us
    pallas_call x1, Pallas kernels: 22.1 us -> 19.8 us  [shards(): pl.pallas_call(functools.partial(route_body, basins, level_count, md, gau...]
where the time goes in v7:
time: 80 us; the launch traced here: 79.8 us
  Pallas kernels  68.7 us (86%)
  starting transfers between devices  5.84 us (7%)
  local copies, waits for them, and re-layouts  1.81 us (2%)
  other arithmetic  1.56 us (2%)
  matrix products  1.11 us (1%)
    pallas_call x1, Pallas kernels, assimilate(): pl.pallas_call(functools.partial(assimilate_body, hours, nb, n, padded),...  28.8 us
    pallas_call x1, Pallas kernels, shards(): pl.pallas_call(functools.partial(route_body, basins, level_count, md, gau...  19.8 us
    pallas_call x1, Pallas kernels, shards(): pl.pallas_call(functools.partial(solve_body, n_member, md), out_shape=jax...  12.7 us
    pallas_call x1, Pallas kernels, exchange(): pl.pallas_call(functools.partial(exchange_body, n), out_shape=(jax.ShapeD...  7.34 us
    ppermute x3, starting transfers between devices, permuted_step(): other = lax.ppermute(held, axis, [(i, i ^ bit) for i in range(n)])  5.84 us
  transfers between devices with their start and end apart: 3, of which 0 were waited for; matrix products, arithmetic and copies ran while one was open for 0% of the time, Pallas kernels for 86%

profile of v7, /device:TPU:0, one launch (start us, length us, event | category | flops | bytes accessed | tf_op | source)
XLA Modules:
  0.0 79.8 jit_solution(17049495569556262931)
XLA Ops:
  0.6 4.1 %collective-permute-start = (f32[1,32,8,128]{3,2,1,0:T(8,128)}, f32[1,32,8,128]{3,2,1,0:T(8,128)S(1)}, u32[]{:S(2)}, u32[]{:S(2)}) collective-permute-start(f32[1,32,8,128]{3,2,1,0:T(8,128)} %bitcast.32), channel_id=1, source_target_pairs={{0,16},{4,20},{8,24},{12,28},{16,0},{20,4},{24,8},{28,12},{1,17},{... | collective-permute-start | bytes 393224 | tf_op jit(solution)/shard_map/ppermute | solution.py:353
  4.8 7.3 %exchange_1.1 = (f32[4,32,8,128]{3,2,1,0:T(8,128)}, s32[4,8,128]{2,1,0:T(8,128)}) custom-call(f32[32,8,128]{2,1,0:T(8,128)} %prior_ref.3, s32[1,128]{1,0:T(1,128)} %bitcast.37, s32[1,128]{1,0:T(1,128)} %bitcast.38, s32[4,128]{1,0:T(4,128)} %bitcast.36), custom_call_target="tpu_custom_call" | custom-call | tf_op jit(solution)/shard_map/exchange_1/pallas_call | solution.py:83
  12.1 0.0 collective-permute-done
  12.1 0.9 %pad_maximum_fusion.2 = f32[2,32,8,128]{3,2,1,0:T(8,128)S(1)} fusion(f32[1,32,8,128]{3,2,1,0:T(8,128)S(1)} %collective-permute-done, f32[1,32,8,128]{3,2,1,0:T(8,128)} %bitcast.33), kind=kLoop, calls=%fused_computation.6 | loop fusion | flops 65536 | bytes 524288 | tf_op jit(solution)/shard_map/concatenate | solution.py:354
  13.0 1.6 %collective-permute-start.1 = (f32[2,32,8,128]{3,2,1,0:T(8,128)S(1)}, f32[2,32,8,128]{3,2,1,0:T(8,128)S(1)}, u32[]{:S(2)}, u32[]{:S(2)}) collective-permute-start(f32[2,32,8,128]{3,2,1,0:T(8,128)S(1)} %pad_maximum_fusion.2), channel_id=1, source_target_pairs={{0,8},{4,12},{8,0},{12,4},{16,24},{20,28},{24,16},{28,20},{1,9},{5... | collective-permute-start | bytes 786440 | tf_op jit(solution)/shard_map/ppermute | solution.py:353
  14.7 19.8 %route.1.x_ref = f32[4,64,512]{2,1,0:T(8,128)} custom-call(s32[1]{0:T(128)} %bitcast.basin_ref, f32[4,32,8,128]{3,2,1,0:T(8,128)} %get-tuple-element.11.coef_ref, s32[4,8,128]{2,1,0:T(8,128)} %get-tuple-element.12.given_ref, f32[32,8,128]{2,1,0:T(8,128)} %prior_ref.3, f32[6,32,128]{2,1,0:T(8,128)} %constant.14.clone.cos_ref, f32[128,128]{1,0:T(8,128)} %bitcast.34, ...), custom_call_target="tpu_custom_call" | custom-call | flops 40000000 | bytes 60000000 | tf_op jit(solution)/shard_map/route/pallas_call | solution.py:622
  34.5 0.0 collective-permute-done.1
  34.6 0.0 copy-start
  34.6 0.1 collective-permute-start.2
  34.7 0.1 reduce_sum.21
  34.8 28.8 %assimilate_2.1 = (f32[32,2,512]{2,1,0:T(2,128)}, f32[288,256]{1,0:T(8,128)}) custom-call(f32[4,64,512]{2,1,0:T(8,128)} %route.1.x_ref, f32[2,512]{1,0:T(2,128)} %obs_ref.1, f32[2,512]{1,0:T(2,128)} %var_ref.1, f32[32,2,512]{2,1,0:T(2,128)} %noise_ref.1), custom_call_target="tpu_custom_call" | custom-call | tf_op jit(solution)/shard_map/assimilate_2/pallas_call | solution.py:325
  63.7 12.7 %solve.1 = f32[256,32]{1,0:T(8,128)} custom-call(f32[288,256]{1,0:T(8,128)} %get-tuple-element.15.sums_ref), custom_call_target="tpu_custom_call" | custom-call | flops 40000000 | bytes 60000000 | tf_op jit(solution)/shard_map/solve/pallas_call | solution.py:655
  76.4 0.0 copy-start.1
  76.4 0.0 copy-start.2
  76.4 0.0 collective-permute-done.2
  76.4 0.1 reduce_sum.22
  76.5 0.1 pad_maximum_fusion
  76.6 0.2 fusion.1
  76.8 0.3 copy.14
  77.2 0.0 copy-done
  77.2 0.1 copy-done.1
  77.3 1.1 %convolution_add_fusion = f32[32,8,128]{2,0,1:T(8,128)S(1)} fusion(f32[8,128,256]{2,1,0:T(8,128)S(1)} %bitcast.31, f32[256,32]{1,0:T(8,128)S(1)} %copy-done.1, f32[32,8,128]{2,1,0:T(8,128)S(1)} %copy-done), kind=kOutput, calls=%fused_computation | convolution fusion | flops 100696064 | bytes 1343488 | tf_op jit(solution)/shard_map/dot_general | solution.py:669
  78.4 0.7 copy.17
  79.1 0.0 copy-done.2
  79.1 0.7 copy.24
  (2 shorter events, 0.0 us)
Async XLA Ops:
  0.6 11.5 %collective-permute-start = (f32[1,32,8,128]{3,2,1,0:T(8,128)}, f32[1,32,8,128]{3,2,1,0:T(8,128)S(1)}, u32[]{:S(2)}, u32[]{:S(2)}) collective-permute-start(f32[1,32,8,128]{3,2,1,0:T(8,128)} %bitcast.32), channel_id=1, source_target_pairs={{0,16},{4,20},{8,24},{12,28},{16,0},{20,4},{24,8},{28,12},{1,17},{... | collective-permute-start | bytes 393224 | tf_op jit(solution)/shard_map/ppermute | solution.py:353
  13.0 21.5 %collective-permute-start.1 = (f32[2,32,8,128]{3,2,1,0:T(8,128)S(1)}, f32[2,32,8,128]{3,2,1,0:T(8,128)S(1)}, u32[]{:S(2)}, u32[]{:S(2)}) collective-permute-start(f32[2,32,8,128]{3,2,1,0:T(8,128)S(1)} %pad_maximum_fusion.2), channel_id=1, source_target_pairs={{0,8},{4,12},{8,0},{12,4},{16,24},{20,28},{24,16},{28,20},{1,9},{5... | collective-permute-start | bytes 786440 | tf_op jit(solution)/shard_map/ppermute | solution.py:353
  34.6 42.6 %copy-start = (f32[32,8,128]{2,1,0:T(8,128)S(1)}, f32[32,8,128]{2,1,0:T(8,128)}, u32[]{:S(2)}) copy-start(f32[32,8,128]{2,1,0:T(8,128)} %prior_ref.3) | copy-start | bytes 393220
  34.6 41.8 %collective-permute-start.2 = (f32[4,32,8,128]{3,2,1,0:T(8,128)S(1)}, f32[4,32,8,128]{3,2,1,0:T(8,128)S(1)}, u32[]{:S(2)}, u32[]{:S(2)}) collective-permute-start(f32[4,32,8,128]{3,2,1,0:T(8,128)S(1)} %pad_maximum_fusion.1), channel_id=1, source_target_pairs={{0,4},{4,0},{8,12},{12,8},{16,20},{20,16},{24,28},{28,24},{1,5},{5... | collective-permute-start | bytes 1572872 | tf_op jit(solution)/shard_map/ppermute | solution.py:353
  76.4 0.9 %copy-start.1 = (f32[256,32]{1,0:T(8,128)S(1)}, f32[256,32]{1,0:T(8,128)}, u32[]{:S(2)}) copy-start(f32[256,32]{1,0:T(8,128)} %solve.1) | copy-start | bytes 98308
  76.4 2.8 %copy-start.2 = (f32[32,2,512]{2,1,0:T(2,128)S(1)}, f32[32,2,512]{2,1,0:T(2,128)}, u32[]{:S(2)}) copy-start(f32[32,2,512]{2,1,0:T(2,128)} %get-tuple-element.23) | copy-start | bytes 393220
